TPU v7x, 128 devices: a whole 4x4x4 slice. The times are simulated.
128 devices in a mesh: row: 8 (over z_lo, x), col: 16 (over z_hi, y, core).
Axes of the slice: x: 4, y: 4, z: 4 (z_hi: 2, z_lo: 2; z = z_hi * 2 + z_lo), core: 2. Of those that a mesh axis runs over, the one named last changes fastest.
Arguments:
- coarse_left: float32 [32, 16384], P('col', 'row'), may hold values from -3 to 3
- coarse_right: float32 [32, 16384], P('row', 'col'), may hold values from -3 to 3
- stencil_left: int32 [65536], P('row'), may hold values from -1 to 16384, as said below
- weights_left: float32 [4, 65536], P(None, 'row'), may hold values from 0.1 to 0.6
- stencil_right: int32 [65536], P('col'), may hold values from -1 to 16384, as said below
- weights_right: float32 [4, 65536], P(None, 'col'), may hold values from 0.1 to 0.6
- tile_mask: int32 [16, 16], P('row', 'col'), may hold values 0 or 1
- sample_rows: int32 [16, 16, 2048], P('row', 'col'), may hold values from 0 to 4095
- sample_cols: int32 [16, 16, 2048], P('row', 'col'), may hold values from 0 to 4095
- sample_values: float32 [16, 16, 2048], P('row', 'col'), may hold values from -6 to 6
Outputs:
- left_new: float32 [32, 65536], P('col', 'row')
- right_new: float32 [32, 65536], P('row', 'col')
Inputs may be any that keep to these rules, and one draw needn't show every extreme that they name: stencil_left[i] is i // 4 - 1, i // 4 or i // 4 + 1. stencil_right[j] is j // 4 - 1, j // 4 or j // 4 + 1.
All inputs are finite; a program needn't handle non-finite values. No bound on the sum of `tile_mask` on one device may be relied on, other than what follows from the above.
Results may differ from a plain program's by a relative error of at most 0.0001.
Values sent between devices are 32-bit elements; how exact they have to be, the bound alone decides.
A program may use at most 64 MiB of HBM per device.

v0:
```python
import jax
import jax.numpy as jnp
from jax import lax
from jax.sharding import PartitionSpec as P

TILES = 16
TILE = 4096
SPT = 2048


def with_halo(block, sides, width):
    for axis, dim in sides:
        count = lax.axis_size(axis)
        forward = [(i, i + 1) for i in range(count - 1)]
        backward = [(target, source) for source, target in forward]
        low = lax.ppermute(
            lax.slice_in_dim(block, block.shape[dim] - width, None, axis=dim), axis, forward
        )
        high = lax.ppermute(lax.slice_in_dim(block, 0, width, axis=dim), axis, backward)
        block = jnp.concatenate([low, block, high], axis=dim)
    return block


def from_everyone(shard, axis):
    copies = jnp.broadcast_to(shard, (lax.axis_size(axis), *shard.shape))
    return lax.all_to_all(copies, axis, split_axis=0, concat_axis=0, tiled=True)


def in_order(parts, dim):
    parts = jnp.moveaxis(parts, 0, dim)
    shape = parts.shape
    return parts.reshape(*shape[:dim], shape[dim] * shape[dim + 1], *shape[dim + 2 :])


def gather_directly(shard, axis, dim):
    parts = from_everyone(shard, axis)
    return in_order(parts, dim)


def split_up(shard, dim, devices):
    shape = shard.shape
    parts = shard.reshape(*shape[:dim], devices, shape[dim] // devices, *shape[dim + 1 :])
    return jnp.moveaxis(parts, dim, 0)


def sum_at_owner(shard, axis, dim):
    devices = lax.axis_size(axis)
    parts = lax.all_to_all(split_up(shard, dim, devices), axis, 0, 0, tiled=True)
    return jnp.sum(parts, axis=0)


def spread(padded, base, weights, offset):
    start_at = base - offset + 2
    columns_at = start_at[None, :] + jnp.arange(4, dtype=jnp.int32)[:, None]
    values = jnp.take(padded, columns_at, axis=1)
    return jnp.sum(values * weights[None], axis=1)


def on_device(
    coarse_left,
    coarse_right,
    stencil_left,
    weights_left,
    stencil_right,
    weights_right,
    tile_mask,
    sample_rows,
    sample_cols,
    sample_values,
):
    left_offset = lax.axis_index("row") * coarse_left.shape[1]
    right_offset = lax.axis_index("col") * coarse_right.shape[1]
    left_padded = with_halo(coarse_left, (("row", 1),), 3)
    left_own = spread(left_padded, stencil_left, weights_left, left_offset)
    fine_left = gather_directly(left_own, "col", 0)
    right_padded = with_halo(coarse_right, (("col", 1),), 3)
    right_own = spread(right_padded, stencil_right, weights_right, right_offset)
    fine_right = gather_directly(right_own, "row", 0)
    tile_rows, tile_cols, samples = sample_rows.shape
    row_base = (jnp.arange(tile_rows, dtype=jnp.int32) * TILE)[:, None, None]
    col_base = (jnp.arange(tile_cols, dtype=jnp.int32) * TILE)[None, :, None]
    count = tile_rows * tile_cols * samples
    width = min(count, 4096)
    blocks = count // width
    rows_all = (sample_rows + row_base).reshape(blocks, width)
    cols_all = (sample_cols + col_base).reshape(blocks, width)
    values_all = sample_values.reshape(blocks, width)
    keeping = jnp.broadcast_to(
        tile_mask[:, :, None].astype(jnp.float32), sample_values.shape
    ).reshape(blocks, width)

    def visit(carry, block):
        grad_left, grad_right = carry
        rows_here, cols_here, values_here, keep_here = block
        left_cols = jnp.take(fine_left, rows_here, axis=1)
        right_cols = jnp.take(fine_right, cols_here, axis=1)
        error = keep_here * (jnp.sum(left_cols * right_cols, axis=0) - values_here)
        grad_left = grad_left.at[:, rows_here].add(error[None, :] * right_cols)
        grad_right = grad_right.at[:, cols_here].add(error[None, :] * left_cols)
        return ((grad_left, grad_right), None)

    left_zero = jnp.zeros(fine_left.shape, jnp.float32)
    right_zero = jnp.zeros(fine_right.shape, jnp.float32)
    (grad_left, grad_right), _ = lax.scan(
        visit, (left_zero, right_zero), (rows_all, cols_all, values_all, keeping)
    )
    left_mine = sum_at_owner(grad_left, "col", 0)
    right_mine = sum_at_owner(grad_right, "row", 0)
    step_size = 4.0 * TILE / (SPT * TILES)
    return (left_own - step_size * left_mine, right_own - step_size * right_mine)


def solution(mesh):
    in_specs = (
        P("col", "row"),
        P("row", "col"),
        P("row"),
        P(None, "row"),
        P("col"),
        P(None, "col"),
        P("row", "col"),
        P("row", "col", None),
        P("row", "col", None),
        P("row", "col", None),
    )
    out_specs = (P("col", "row"), P("row", "col"))
    return jax.shard_map(
        on_device, mesh=mesh, in_specs=in_specs, out_specs=out_specs, check_vma=False
    )
```

profile of v0, /device:TPU:0, one launch (start us, length us, event | category | flops | bytes accessed | tf_op | source)
XLA Modules:
  0.0 357.0 jit_solution(8916964457263838409)
XLA Ops:
  1.4 3.5 collective-permute-start
  4.9 1.3 collective-permute-start.1
  6.2 0.8 fusion.23
  7.0 1.4 collective-permute-start.2
  8.4 1.3 collective-permute-start.3
  11.5 0.8 broadcast_add_fusion
  12.4 0.8 concatenate.6
  13.6 108.4 %gather_fusion = f32[32768,2]{1,0:T(8,128)} fusion(f32[2,2054]{0,1:T(8,128)S(1)} %copy.54, s32[32768]{0:T(1024)S(1)} %broadcast_clamp_fusion), kind=kCustom, calls=%fused_computation | custom fusion | bytes 655360 | tf_op jit(solution)/shard_map/jit(_take)/gather | solution.py:55
  122.4 54.5 %gather_fusion.2 = f32[16384,4]{1,0:T(8,128)} fusion(f32[4,1030]{0,1:T(8,128)S(1)} %copy.57, s32[16384]{0:T(1024)S(1)} %broadcast_clamp_fusion.1), kind=kCustom, calls=%fused_computation.2 | custom fusion | bytes 589824 | tf_op jit(solution)/shard_map/jit(_take)/gather | solution.py:55
  176.9 6.9 %multiply_reduce_fusion.1 = f32[4096,4]{1,0:T(8,128)S(1)} fusion(f32[4,4096,4]{2,1,0:T(8,128)} %bitcast.25, f32[4,4096]{1,0:T(4,128)S(1)} %copy-done.2, pred[4,4096]{1,0:T(4,128)(4,1)S(1)} %fusion.21), kind=kLoop, calls=%fused_computation.7 | loop fusion | flops 180224 | bytes 409600 | tf_op jit(solution)/shard_map/reduce_sum | solution.py:56
  184.5 0.9 broadcast_in_dim.83
  185.3 6.6 %all-to-all-start.1 = ((f32[8,4,4096]{2,1,0:T(4,128)}), f32[8,4,4096]{2,1,0:T(4,128)S(1)}, u32[]{:S(2)}, u32[]{:S(2)}) async-start(f32[8,4,4096]{2,1,0:T(4,128)} %broadcast_in_dim.83), calls=%async_computation.1 | async-start | bytes 1048576 | tf_op jit(solution)/shard_map/all_to_all | solution.py:26
  192.0 14.8 %multiply_reduce_fusion = f32[8192,2]{1,0:T(8,128)} fusion(f32[4,8192,2]{2,1,0:T(8,128)} %bitcast.24, f32[4,8192]{1,0:T(4,128)S(1)} %copy-done.1, pred[4,8192]{1,0:T(4,128)(4,1)S(1)} %fusion.17), kind=kLoop, calls=%fused_computation.6 | loop fusion | flops 180224 | bytes 491520 | tf_op jit(solution)/shard_map/reduce_sum | solution.py:56
  206.7 2.8 copy.55
  209.6 1.4 broadcast_in_dim.78
  211.0 11.6 %all-to-all-start = ((f32[16,2,8192]{2,1,0:T(2,128)}), f32[16,2,8192]{2,1,0:T(2,128)S(1)}, u32[]{:S(2)}, u32[]{:S(2)}) async-start(f32[16,2,8192]{2,1,0:T(2,128)} %broadcast_in_dim.78), calls=%async_computation | async-start | bytes 2097152 | tf_op jit(solution)/shard_map/all_to_all | solution.py:26
  222.7 1.0 reshape.227
  223.6 1.6 copy.59
  225.3 14.1 %gather_fusion.3 = f32[4096,32]{1,0:T(8,128)} fusion(f32[32,4096]{0,1:T(8,128)S(1)} %copy.59, s32[4096]{0:T(1024)S(1)} %broadcast_clamp_fusion.2), kind=kCustom, calls=%fused_computation.3 | custom fusion | bytes 1064960 | tf_op jit(solution)/shard_map/while/body/eval_jaxpr/jit(_take)/gather | solution.py:96
  239.4 1.1 all-to-all-done
  241.2 2.6 copy.56
  243.9 16.4 %gather_fusion.1 = f32[4096,32]{1,0:T(8,128)} fusion(f32[32,8192]{0,1:T(8,128)} %copy.56, s32[4096]{0:T(1024)S(1)} %broadcast_clamp_fusion.3), kind=kCustom, calls=%fused_computation.1 | custom fusion | bytes 1064960 | tf_op jit(solution)/shard_map/while/body/eval_jaxpr/jit(_take)/gather | solution.py:95
  260.3 3.7 %multiply_reduce_fusion.2 = f32[4096]{0:T(1024)S(1)} fusion(f32[4096,32]{1,0:T(8,128)S(1)} %copy-done, f32[4096,32]{1,0:T(8,128)} %gather_fusion.1, pred[4096]{0:T(1024)(128)(4,1)S(1)} %get-tuple-element.37, pred[4096]{0:T(1024)(128)(4,1)S(1)} %get-tuple-element.38), kind=kLoop, calls=%fused_computation.12 | loop fusion | flops 520192 | bytes 1073152 | tf_op jit(solution)/shard_map/while/body/eval_jaxpr/reduce_sum | solution.py:97
  264.1 27.1 %scatter_custom_fusion.1 = f32[32,4096]{0,1:T(8,128)} fusion(s32[4096]{0:T(1024)S(1)} %bitcast.37, f32[4096,32]{1,0:T(8,128)} %gather_fusion.1, f32[4096]{0:T(1024)S(1)} %subtract_multiply_fusion, f32[]{:T(128)} %constant.93.clone.1, f32[]{:T(128)} %constant.94.clone.1, pred[4096]{0:T(1024)(128)(4,1)S(1)} %get-tuple-element.38), kind=kCustom, calls=%fused_computation.8 | custom fusion | flops 393216 | bytes 1069064 | tf_op jit(solution)/shard_map/while/body/eval_jaxpr/scatter-add | solution.py:99
  291.2 2.2 copy.61
  293.3 1.0 reshape.229
  294.3 5.1 %all-to-all-start.3 = ((f32[8,4,4096]{2,1,0:T(4,128)}), f32[8,4,4096]{2,1,0:T(4,128)S(1)}, u32[]{:S(2)}, u32[]{:S(2)}) async-start(f32[8,4,4096]{2,1,0:T(4,128)} %reshape.229), calls=%async_computation.3 | async-start | bytes 1048576 | tf_op jit(solution)/shard_map/all_to_all | solution.py:48
  299.4 27.4 %scatter_custom_fusion = f32[32,8192]{0,1:T(8,128)} fusion(s32[4096]{0:T(1024)S(1)} %bitcast.35, f32[]{:T(128)} %constant.94.clone.1, f32[4096,32]{1,0:T(8,128)S(1)} %copy-done, f32[4096]{0:T(1024)S(1)} %subtract_multiply_fusion, f32[]{:T(128)} %constant.93.clone.1, pred[4096]{0:T(1024)(128)(4,1)S(1)} %get-tuple-element.37), kind=kCustom, calls=%fused_computation.10 | custom fusion | flops 393216 | bytes 3166216 | tf_op jit(solution)/shard_map/while/body/eval_jaxpr/scatter-add | solution.py:98
  326.8 2.8 copy.60
  329.6 1.6 reshape.228
  331.2 6.7 %all-to-all-start.2 = ((f32[16,2,8192]{2,1,0:T(2,128)}), f32[16,2,8192]{2,1,0:T(2,128)S(1)}, u32[]{:S(2)}, u32[]{:S(2)}) async-start(f32[16,2,8192]{2,1,0:T(2,128)} %reshape.228), calls=%async_computation.2 | async-start | bytes 2097152 | tf_op jit(solution)/shard_map/all_to_all | solution.py:48
  338.7 17.2 %all-to-all-done.2 = f32[16,2,8192]{2,1,0:T(2,128)S(1)} async-done(((f32[16,2,8192]{2,1,0:T(2,128)}), f32[16,2,8192]{2,1,0:T(2,128)S(1)}, u32[]{:S(2)}, u32[]{:S(2)}) %all-to-all-start.2) | async-done | bytes 1048608 | tf_op jit(solution)/shard_map/all_to_all | solution.py:48
  (49 shorter events, 6.5 us)
Async XLA Ops:
  1.4 11.0 %collective-permute-start = (f32[2,3]{1,0:T(2,128)S(1)}, f32[2,3]{1,0:T(2,128)S(1)}, u32[]{:S(2)}, u32[]{:S(2)}) collective-permute-start(f32[2,3]{1,0:T(2,128)S(1)} %get-tuple-element.25), channel_id=1, source_target_pairs={{0,16},{16,32},{32,48},{48,64},{64,80},{80,96},{96,112},{1,17},{17... | collective-permute-start | bytes 80 | tf_op jit(solution)/shard_map/ppermute | solution.py:16
  4.9 7.5 %collective-permute-start.1 = (f32[2,3]{1,0:T(2,128)S(1)}, f32[2,3]{1,0:T(2,128)S(1)}, u32[]{:S(2)}, u32[]{:S(2)}) collective-permute-start(f32[2,3]{1,0:T(2,128)S(1)} %get-tuple-element.24), channel_id=1, source_target_pairs={{16,0},{32,16},{48,32},{64,48},{80,64},{96,80},{112,96},{17,1},{33... | collective-permute-start | bytes 80 | tf_op jit(solution)/shard_map/ppermute | solution.py:19
  7.0 115.1 %collective-permute-start.2 = (f32[4,3]{1,0:T(4,128)S(1)}, f32[4,3]{1,0:T(4,128)S(1)}, u32[]{:S(2)}, u32[]{:S(2)}) collective-permute-start(f32[4,3]{1,0:T(4,128)S(1)} %get-tuple-element.36), channel_id=1, source_target_pairs={{0,1},{1,2},{2,3},{3,4},{4,5},{5,6},{6,7},{7,8},{8,9},{9,10},{10,1... | collective-permute-start | bytes 152 | tf_op jit(solution)/shard_map/ppermute | solution.py:16
  8.4 113.6 %collective-permute-start.3 = (f32[4,3]{1,0:T(4,128)S(1)}, f32[4,3]{1,0:T(4,128)S(1)}, u32[]{:S(2)}, u32[]{:S(2)}) collective-permute-start(f32[4,3]{1,0:T(4,128)S(1)} %get-tuple-element.26), channel_id=1, source_target_pairs={{1,0},{2,1},{3,2},{4,3},{5,4},{6,5},{7,6},{8,7},{9,8},{10,9},{11,1... | collective-permute-start | bytes 152 | tf_op jit(solution)/shard_map/ppermute | solution.py:19
  11.5 110.6 %copy-start.4 = (f32[4,1024]{1,0:T(4,128)S(1)}, f32[4,1024]{1,0:T(4,128)}, u32[]{:S(2)}) copy-start(f32[4,1024]{1,0:T(4,128)} %param.11) | copy-start | bytes 49156
  122.0 54.9 %copy-start.2 = (f32[4,4096]{1,0:T(4,128)S(1)}, f32[4,4096]{1,0:T(4,128)}, u32[]{:S(2)}) copy-start(f32[4,4096]{1,0:T(4,128)} %param.15) | copy-start | bytes 196612
  183.8 8.1 %copy-start.1 = (f32[4,8192]{1,0:T(4,128)S(1)}, f32[4,8192]{1,0:T(4,128)}, u32[]{:S(2)}) copy-start(f32[4,8192]{1,0:T(4,128)} %param.13) | copy-start | bytes 393220
  185.3 24.3 %all-to-all-start.1 = ((f32[8,4,4096]{2,1,0:T(4,128)}), f32[8,4,4096]{2,1,0:T(4,128)S(1)}, u32[]{:S(2)}, u32[]{:S(2)}) async-start(f32[8,4,4096]{2,1,0:T(4,128)} %broadcast_in_dim.83), calls=%async_computation.1 | async-start | bytes 1048576 | tf_op jit(solution)/shard_map/all_to_all | solution.py:26
  209.6 13.0 %copy-start.3 = (s32[2,1,2048]{2,1,0:T(1,128)S(1)}, s32[2,1,2048]{2,1,0:T(1,128)}, u32[]{:S(2)}) copy-start(s32[2,1,2048]{2,1,0:T(1,128)} %param.18) | copy-start | bytes 49156
  209.6 13.0 %copy-start.6 = (s32[2,1]{0,1:T(1,128)S(1)}, s32[2,1]{0,1:T(1,128)}, u32[]{:S(2)}) copy-start(s32[2,1]{0,1:T(1,128)} %param.16) | copy-start | bytes 28
  211.0 29.5 %all-to-all-start = ((f32[16,2,8192]{2,1,0:T(2,128)}), f32[16,2,8192]{2,1,0:T(2,128)S(1)}, u32[]{:S(2)}, u32[]{:S(2)}) async-start(f32[16,2,8192]{2,1,0:T(2,128)} %broadcast_in_dim.78), calls=%async_computation | async-start | bytes 2097152 | tf_op jit(solution)/shard_map/all_to_all | solution.py:26
  243.9 16.4 %copy-start = (f32[4096,32]{1,0:T(8,128)S(1)}, f32[4096,32]{1,0:T(8,128)}, u32[]{:S(2)}) copy-start(f32[4096,32]{1,0:T(8,128)} %gather_fusion.3) | copy-start | bytes 1572868
  260.3 3.8 %copy-start.5 = (f32[2,1,2048]{2,1,0:T(1,128)S(1)}, f32[2,1,2048]{2,1,0:T(1,128)}, u32[]{:S(2)}) copy-start(f32[2,1,2048]{2,1,0:T(1,128)} %param.19) | copy-start | bytes 49156
  294.3 36.9 %all-to-all-start.3 = ((f32[8,4,4096]{2,1,0:T(4,128)}), f32[8,4,4096]{2,1,0:T(4,128)S(1)}, u32[]{:S(2)}, u32[]{:S(2)}) async-start(f32[8,4,4096]{2,1,0:T(4,128)} %reshape.229), calls=%async_computation.3 | async-start | bytes 1048576 | tf_op jit(solution)/shard_map/all_to_all | solution.py:48
  331.2 24.7 %all-to-all-start.2 = ((f32[16,2,8192]{2,1,0:T(2,128)}), f32[16,2,8192]{2,1,0:T(2,128)S(1)}, u32[]{:S(2)}, u32[]{:S(2)}) async-start(f32[16,2,8192]{2,1,0:T(2,128)} %reshape.228), calls=%async_computation.2 | async-start | bytes 2097152 | tf_op jit(solution)/shard_map/all_to_all | solution.py:48
where the time goes:
time: 358 us; the launch traced here: 357 us
  local copies, waits for them, and re-layouts  216 us (60%)
  other arithmetic  84.3 us (24%)
  starting transfers between devices  37.5 us (10%)
  waiting for transfers between devices  18.3 us (5%)
    gather x2, local copies, waits for them, and re-layouts, spread(): values = jnp.take(padded, columns_at, axis=1)  163 us
    scatter-add x1, other arithmetic, visit(): grad_left = grad_left.at[:, rows_here].add(error[None, :] * right_cols)  27.4 us
    scatter-add x1, other arithmetic, visit(): grad_right = grad_right.at[:, cols_here].add(error[None, :] * left_cols)  27.1 us
    reduce_sum x2, other arithmetic, spread(): return jnp.sum(values * weights[None], axis=1)  21.7 us
    all_to_all x2, starting transfers between devices, from_everyone(): return lax.all_to_all(copies, axis, split_axis=0, concat_axis=0, tiled=True)  18.2 us
    all_to_all x2, waiting for transfers between devices, sum_at_owner(): lax.all_to_all(split_up(shard, dim, devices), axis, 0, 0, tiled=True)  17.2 us
    gather x1, local copies, waits for them, and re-layouts, visit(): left_cols = jnp.take(fine_left, rows_here, axis=1)  16.4 us
    gather x1, local copies, waits for them, and re-layouts, visit(): right_cols = jnp.take(fine_right, cols_here, axis=1)  14.1 us
  transfers between devices with their start and end apart: 8, of which 2 were waited for; matrix products, arithmetic and copies ran while one was open for 50% of the time, Pallas kernels for 0%

commit v1 on v0

v1 whole, which is shorter than its diff:
```python
import functools
import jax, jax.numpy as jnp
from jax import lax
from jax.sharding import PartitionSpec as P
from jax.experimental import pallas as pl
from jax.experimental.pallas import tpu as pltpu

TILE = 4096
SPT = 2048
LANES = 128
ETA = 0.5
f32, bf16, i32 = jnp.float32, jnp.bfloat16, jnp.int32


def lane_pick(table, index):
    return jnp.take_along_axis(table, index, axis=1)


def interpolate(coarse_ref, stencil_ref, weight_ref, fine_ref, origin, blocks):
    rank = coarse_ref.shape[0]
    groups = rank // 8

    @pl.loop(0, blocks)
    def _(b):
        at = pl.multiple_of(b * 128, 128)
        before = coarse_ref[:, pl.ds(at, 128)]
        here = coarse_ref[:, pl.ds(at + 128, 128)]
        after = coarse_ref[:, pl.ds(at + 256, 128)]
        low = jnp.concatenate([before[:, 64:], here[:, :64]], axis=1)
        high = jnp.concatenate([here[:, 64:], after[:, :64]], axis=1)
        for q, (window, shift) in enumerate(((low, 64), (here, 0), (here, 0), (high, -64))):
            fine_at = pl.multiple_of(b * 512 + q * 128, 128)
            base = stencil_ref[:, pl.ds(fine_at, 128)] - (origin + b * 128 - shift + 1)
            for g in range(groups):
                total = None
                for t in range(4):
                    index = jnp.broadcast_to(base + t, (8, 128))
                    picked = lane_pick(window[8 * g : 8 * g + 8], index)
                    term = picked * weight_ref[t : t + 1, pl.ds(fine_at, 128)]
                    total = term if total is None else total + term
                fine_ref[8 * g : 8 * g + 8, pl.ds(fine_at, 128)] = total


def pick_columns(fine_ref, start, position):
    hi = jnp.broadcast_to(position // 128, (8, 128))
    lo = jnp.broadcast_to(position % 128, (8, 128))
    got = [None] * 4
    for j in range(TILE // 128):
        mask = hi == j
        column = pl.multiple_of(start + j * 128, 128)
        for g in range(4):
            p = lane_pick(fine_ref[8 * g : 8 * g + 8, pl.ds(column, 128)], lo)
            got[g] = p if got[g] is None else jnp.where(mask, p, got[g])
    return got


def sublane_pick(x, first, period):
    index = first + lax.broadcasted_iota(i32, (8, 128), 0) % period
    return jnp.take_along_axis(x, index, axis=0)


def build_side(values, position, period, lhs_ref, ohot_ref, at, width):
    j = position // 128
    lane = position % 128
    half = 8 // period
    sel = (j // half) % 2
    hi = (j // (2 * half)) * half + j % half
    lo = sel * 128 + lane
    parts = 16 // (16 // period)
    row16 = lax.broadcasted_iota(i32, (16, 128), 0)
    tall = 16 // (16 // period)
    hi16 = jnp.broadcast_to(hi, (16, 128))
    per_tile = 16 // period
    masks = [
        jnp.where(hi16 == m * per_tile + row16 // period, 1.0, 0.0).astype(bf16)
        for m in range(16 // per_tile)
    ]
    slot_rows = 16 * len(masks)
    slot = 0
    for g in range(4):
        for first in range(0, 8, period):
            dup = sublane_pick(values[g], first, period)
            dup = jnp.concatenate([dup, dup], axis=0)
            top = dup.astype(bf16)
            rest = (dup - top.astype(f32)).astype(bf16)
            for m, mask in enumerate(masks):
                rows = slice(slot * slot_rows + 16 * m, slot * slot_rows + 16 * m + 16)
                lhs_ref[rows, pl.ds(at, 128)] = top * mask
                lhs_ref[rows, pl.ds(at + width, 128)] = rest * mask
            slot += 1
    lo256 = jnp.broadcast_to(lo, (256, 128))
    hot = jnp.where(lo256 == lax.broadcasted_iota(i32, (256, 128), 0), 1.0, 0.0).astype(bf16)
    ohot_ref[:, pl.ds(at, 128)] = hot
    ohot_ref[:, pl.ds(at + width, 128)] = hot


def add_side(lhs_ref, ohot_ref, out_ref, period, at):
    got = lax.dot_general(
        lhs_ref[...], ohot_ref[...], (((1,), (1,)), ((), ())), preferred_element_type=f32
    )
    slots = 32 // period
    groups = 64 // slots
    for slot in range(slots):
        for g in range(groups):
            for h in range(2):
                row = (slot * groups + g) * 8
                rows = pl.ds(pl.multiple_of(at + g * 16 + h * 8, 8), 8)
                out_ref[slot, rows, :] += got[row : row + 8, h * 128 : h * 128 + 128]


def add_own(fine_ref, out_ref, slot, period):
    group = pl.multiple_of((slot * period) // 8 * 8, 8)
    row = lax.broadcasted_iota(i32, (8, 128), 0)
    index = (slot * period) % 8 + row % period
    spread = 8 // period

    @pl.loop(0, 128 // 8)
    def _(block):
        got = None
        for q in range(spread):
            lanes = pl.ds(pl.multiple_of((block * spread + q) * 128, 128), 128)
            picked = jnp.take_along_axis(fine_ref[pl.ds(group, 8), lanes], index, axis=0)
            got = picked if got is None else jnp.where(row // period == q, picked, got)
        out_ref[slot, pl.ds(pl.multiple_of(block * 8, 8), 8), :] += got


CHUNK = 512


def local_kernel(
    mask_ref, left_ref, right_ref, sl_ref, wl_ref, sr_ref, wr_ref, rows_ref, cols_ref, vals_ref,
    ol_ref, or_ref, fl_ref, fr_ref, lhs_ref, ohot_ref,
):
    my_row = lax.axis_index("row")
    my_col = lax.axis_index("col")
    interpolate(left_ref, sl_ref, wl_ref, fl_ref, my_row * 2048, 16)
    interpolate(right_ref, sr_ref, wr_ref, fr_ref, my_col * 1024, 8)
    ol_ref[...] = jnp.zeros(ol_ref.shape, f32)
    or_ref[...] = jnp.zeros(or_ref.shape, f32)

    per_tile = SPT // CHUNK

    @pl.loop(0, 2 * per_tile)
    def _(step):
        tile = step // per_tile
        first = (step % per_tile) * CHUNK
        keep = mask_ref[tile, 0].astype(f32) * -ETA

        @pl.loop(0, CHUNK // 128)
        def _(sub):
            at = pl.multiple_of(sub * 128, 128)
            s_at = pl.multiple_of(first + sub * 128, 128)
            row = rows_ref[tile, :, pl.ds(s_at, 128)]
            col = cols_ref[tile, :, pl.ds(s_at, 128)]
            left = pick_columns(fl_ref, tile * TILE, row)
            right = pick_columns(fr_ref, 0, col)
            dots = sum(left[g] * right[g] for g in range(4))
            error = jnp.sum(dots, axis=0, keepdims=True) - vals_ref[tile, :, pl.ds(s_at, 128)]
            scaled = error * keep
            build_side([scaled * right[g] for g in range(4)], row, 2, lhs_ref.at[0], ohot_ref.at[0], at, CHUNK)
            build_side([scaled * left[g] for g in range(4)], col, 4, lhs_ref.at[1], ohot_ref.at[1], at, CHUNK)

        add_side(lhs_ref.at[0], ohot_ref.at[0], ol_ref, 2, tile * 64)
        add_side(lhs_ref.at[1], ohot_ref.at[1], or_ref, 4, 0)

    add_own(fl_ref, ol_ref, my_col, 2)
    add_own(fr_ref, or_ref, my_row, 4)


def local_step(mask, left, right, sl, wl, sr, wr, rows, cols, vals):
    vmem = pl.BlockSpec(memory_space=pltpu.VMEM)
    return pl.pallas_call(
        local_kernel,
        out_shape=(
            jax.ShapeDtypeStruct((16, 128, 128), f32),
            jax.ShapeDtypeStruct((8, 128, 128), f32),
        ),
        in_specs=[pl.BlockSpec(memory_space=pltpu.SMEM)] + [vmem] * 9,
        out_specs=(vmem, vmem),
        scratch_shapes=[
            pltpu.VMEM((32, 8192), f32),
            pltpu.VMEM((32, 4096), f32),
            pltpu.VMEM((2, 512, 2 * CHUNK), bf16),
            pltpu.VMEM((2, 256, 2 * CHUNK), bf16),
        ],
        name="local_step",
    )(mask, left, right, sl.reshape(1, -1), wl, sr.reshape(1, -1), wr, rows, cols, vals)


def with_halo(block, axis):
    count = lax.axis_size(axis)
    forward = [(i, i + 1) for i in range(count - 1)]
    backward = [(i + 1, i) for i in range(count - 1)]
    low = lax.ppermute(block[:, -128:], axis, forward)
    high = lax.ppermute(block[:, :128], axis, backward)
    return jnp.concatenate([low, block, high], axis=1)


def sum_at_owner(parts, axis):
    return jnp.sum(lax.all_to_all(parts, axis, 0, 0, tiled=True), axis=0)


def on_device(coarse_left, coarse_right, sl, wl, sr, wr, mask, rows, cols, vals):
    left = lax.all_gather(with_halo(coarse_left, "row"), "col", axis=0, tiled=True)
    right = lax.all_gather(with_halo(coarse_right, "col"), "row", axis=0, tiled=True)
    gl, gr = local_step(mask, left, right, sl, wl, sr, wr, rows, cols, vals)
    left_new = sum_at_owner(gl, "col").reshape(64, 2, 128).transpose(1, 0, 2).reshape(2, 8192)
    right_new = sum_at_owner(gr, "row").reshape(32, 4, 128).transpose(1, 0, 2).reshape(4, 4096)
    return left_new, right_new


def solution(mesh):
    in_specs = (
        P("col", "row"),
        P("row", "col"),
        P("row"),
        P(None, "row"),
        P("col"),
        P(None, "col"),
        P("row", "col"),
        P("row", "col", None),
        P("row", "col", None),
        P("row", "col", None),
    )
    out_specs = (P("col", "row"), P("row", "col"))
    return jax.shard_map(
        on_device, mesh=mesh, in_specs=in_specs, out_specs=out_specs, check_vma=False
    )
```

time: 358 us -> 139 us (0.39)
  local copies, waits for them, and re-layouts: 216 us -> 3.73 us
  other arithmetic: 84.3 us -> 1.36 us
  blocking collectives: 0 us -> 71.5 us
  Pallas kernels: 0 us -> 30.9 us
  starting transfers between devices: 37.5 us -> 12.3 us
    gather x4 -> x0, local copies, waits for them, and re-layouts: 193 us -> none  [the longest x2 163 us: spread(): values = jnp.take(padded, columns_at, axis=1)]
    all_gather x0 -> x2, blocking collectives: none -> 58.2 us  [the longest x1 29.3 us: on_device(): lax.all_gather(with_halo(coarse_right, 'col'), 'row', axis=0, tiled=True)]
    scatter-add x2 -> x0, other arithmetic: 54.5 us -> none  [the longest x1 27.4 us: visit(): grad_left = grad_left.at[:, rows_here].add(error[None, :] * right_cols)]
    pallas_call x0 -> x1, Pallas kernels: none -> 30.9 us  [local_step(): pl.pallas_call(local_kernel, out_shape=(jax.ShapeDtypeStruct((16, 128, 12...]
    all_to_all x4 -> x1, starting transfers between devices: 30 us -> 4.61 us  [sum_at_owner(): return jnp.sum(lax.all_to_all(parts, axis, 0, 0, tiled=True), axis=0)]
    reduce_sum x5 -> x2, other arithmetic: 25.8 us -> 1.34 us  [sum_at_owner(): return jnp.sum(lax.all_to_all(parts, axis, 0, 0, tiled=True), axis=0)]
    all_to_all x0 -> x1, blocking collectives: none -> 13.3 us  [sum_at_owner(): return jnp.sum(lax.all_to_all(parts, axis, 0, 0, tiled=True), axis=0)]
    reshape x6 -> x0, local copies, waits for them, and re-layouts: 8.54 us -> none  [the longest x4 5.98 us: in_order(): parts.reshape(*shape[:dim], shape[dim] * shape[dim + 1], *shape[dim + 2:])]
  transfers between devices with their start and end apart: 8 -> 5, of which waited for: 2 -> 1; matrix products, arithmetic and copies ran while one was open for 50% -> 2% of each run, Pallas kernels for 0% -> 0%
where the time goes in v1:
time: 139 us; the launch traced here: 138 us
  blocking collectives  71.5 us (51%)
  Pallas kernels  30.9 us (22%)
  waiting for transfers between devices  17.3 us (12%)
  starting transfers between devices  12.3 us (9%)
  local copies, waits for them, and re-layouts  3.73 us (3%)
    pallas_call x1, Pallas kernels, local_step(): pl.pallas_call(local_kernel, out_shape=(jax.ShapeDtypeStruct((16, 128, 12...  30.9 us
    all_gather x1, blocking collectives, on_device(): lax.all_gather(with_halo(coarse_right, 'col'), 'row', axis=0, tiled=True)  29.3 us
    all_gather x1, blocking collectives, on_device(): lax.all_gather(with_halo(coarse_left, 'row'), 'col', axis=0, tiled=True)  28.9 us
    all_to_all x1, waiting for transfers between devices, sum_at_owner(): return jnp.sum(lax.all_to_all(parts, axis, 0, 0, tiled=True), axis=0)  17.3 us
    all_to_all x1, blocking collectives, sum_at_owner(): return jnp.sum(lax.all_to_all(parts, axis, 0, 0, tiled=True), axis=0)  13.3 us
    ppermute x2, starting transfers between devices, with_halo(): low = lax.ppermute(block[:, -128:], axis, forward)  5.07 us
    all_to_all x1, starting transfers between devices, sum_at_owner(): return jnp.sum(lax.all_to_all(parts, axis, 0, 0, tiled=True), axis=0)  4.61 us
  transfers between devices with their start and end apart: 5, of which 1 were waited for; matrix products, arithmetic and copies ran while one was open for 2% of the time, Pallas kernels for 0%

profile of v1, /device:TPU:0, one launch (start us, length us, event | category | flops | bytes accessed | tf_op | source)
XLA Modules:
  0.0 137.7 jit_solution(995299258004594563)
XLA Ops:
  0.6 0.0 copy-start.1
  0.6 0.7 fusion.1
  1.4 3.5 %collective-permute-start = (f32[2,128]{1,0:T(2,128)S(1)}, f32[2,128]{1,0:T(2,128)S(1)}, u32[]{:S(2)}, u32[]{:S(2)}) collective-permute-start(f32[2,128]{1,0:T(2,128)S(1)} %get-tuple-element.8), channel_id=1, source_target_pairs={{0,16},{16,32},{32,48},{48,64},{64,80},{80,96},{96,112},{1,17},{17... | collective-permute-start | bytes 3080 | tf_op jit(solution)/shard_map/ppermute | solution.py:194
  4.9 1.3 collective-permute-start.1
  6.2 0.7 fusion
  6.9 0.0 copy-start.2
  6.9 1.6 %collective-permute-start.2 = (f32[4,128]{1,0:T(4,128)S(1)}, f32[4,128]{1,0:T(4,128)S(1)}, u32[]{:S(2)}, u32[]{:S(2)}) collective-permute-start(f32[4,128]{1,0:T(4,128)S(1)} %get-tuple-element.6), channel_id=1, source_target_pairs={{0,1},{1,2},{2,3},{3,4},{4,5},{5,6},{6,7},{7,8},{8,9},{9,10},{10,1... | collective-permute-start | bytes 6152 | tf_op jit(solution)/shard_map/ppermute | solution.py:194
  8.5 1.3 collective-permute-start.3
  9.8 0.0 copy-done.2
  9.8 0.6 copy.14.mask_ref
  10.4 0.0 collective-permute-done
  10.4 0.0 collective-permute-done.1
  10.4 0.0 copy-done.1
  10.5 28.9 %all-gather = f32[16,2,2304]{2,1,0:T(2,128)S(1)} all-gather(f32[1,2,2304]{2,1,0:T(2,128)S(1)} %maximum_bitcast_fusion.1), channel_id=1, replica_groups=mesh['row'=8,'col'=16] {'col'}, dimensions={0}, use_global_device_ids=true | all-gather | bytes 313344 | tf_op jit(solution)/shard_map/all_gather | solution.py:204
  39.3 0.0 copy-start
  39.3 0.9 reshape.29.left_ref
  40.2 0.0 collective-permute-done.2
  40.2 0.0 collective-permute-done.3
  40.2 0.0 copy-done
  40.3 29.3 %all-gather.1 = f32[8,4,1280]{2,1,0:T(4,128)S(1)} all-gather(f32[1,4,1280]{2,1,0:T(4,128)S(1)} %maximum_bitcast_fusion), channel_id=1, replica_groups=mesh['row'=8,'col'=16] {'row'}, dimensions={0}, use_global_device_ids=true | all-gather | bytes 184320 | tf_op jit(solution)/shard_map/all_gather | solution.py:205
  69.6 0.7 reshape.31.right_ref
  70.3 30.9 %local_step.1 = (f32[16,128,128]{2,1,0:T(8,128)}, f32[8,128,128]{2,1,0:T(8,128)}) custom-call(s32[2,1]{1,0:T(2,128)} %copy.14.mask_ref, f32[32,2304]{1,0:T(8,128)} %reshape.29.left_ref, f32[32,1280]{1,0:T(8,128)} %reshape.31.right_ref, s32[1,8192]{1,0:T(1,128)} %bitcast.18, f32[4,8192]{1,0:T(4,128)} %wl_ref.1, s32[1,4096]{1,0:T(1,128)} %bitcast.19, ...), custom_call_target="tpu_custom_call" | custom-call | tf_op jit(solution)/shard_map/local_step/pallas_call | solution.py:172
  101.2 13.3 %all_to_all.10 = f32[8,128,128]{2,1,0:T(8,128)S(1)} all-to-all(f32[8,128,128]{2,1,0:T(8,128)} %get-tuple-element.5), channel_id=1, replica_groups=mesh['row'=8,'col'=16] {'row'}, dimensions={0} | all-to-all | bytes 1048576 | tf_op jit(solution)/shard_map/all_to_all | solution.py:200
  114.5 4.6 %all-to-all-start = ((f32[16,128,128]{2,1,0:T(8,128)}), f32[16,128,128]{2,1,0:T(8,128)S(1)}, u32[]{:S(2)}, u32[]{:S(2)}) async-start(f32[16,128,128]{2,1,0:T(8,128)} %get-tuple-element.4), calls=%async_computation | async-start | bytes 2097152 | tf_op jit(solution)/shard_map/all_to_all | solution.py:200
  119.1 0.7 reduce_sum.19
  119.8 17.3 %all-to-all-done = f32[16,128,128]{2,1,0:T(8,128)S(1)} async-done(((f32[16,128,128]{2,1,0:T(8,128)}), f32[16,128,128]{2,1,0:T(8,128)S(1)}, u32[]{:S(2)}, u32[]{:S(2)}) %all-to-all-start) | async-done | bytes 1048608 | tf_op jit(solution)/shard_map/all_to_all | solution.py:200
  137.1 0.7 reduce_sum.18
  (2 shorter events, 0.0 us)
Async XLA Ops:
  0.6 9.8 %copy-start.1 = (f32[2,2048]{1,0:T(2,128)S(1)}, f32[2,2048]{1,0:T(2,128)}, u32[]{:S(2)}) copy-start(f32[2,2048]{1,0:T(2,128)} %param.10) | copy-start | bytes 49156
  1.4 9.1 %collective-permute-start = (f32[2,128]{1,0:T(2,128)S(1)}, f32[2,128]{1,0:T(2,128)S(1)}, u32[]{:S(2)}, u32[]{:S(2)}) collective-permute-start(f32[2,128]{1,0:T(2,128)S(1)} %get-tuple-element.8), channel_id=1, source_target_pairs={{0,16},{16,32},{32,48},{48,64},{64,80},{80,96},{96,112},{1,17},{17... | collective-permute-start | bytes 3080 | tf_op jit(solution)/shard_map/ppermute | solution.py:194
  4.9 5.6 %collective-permute-start.1 = (f32[2,128]{1,0:T(2,128)S(1)}, f32[2,128]{1,0:T(2,128)S(1)}, u32[]{:S(2)}, u32[]{:S(2)}) collective-permute-start(f32[2,128]{1,0:T(2,128)S(1)} %get-tuple-element.9), channel_id=1, source_target_pairs={{16,0},{32,16},{48,32},{64,48},{80,64},{96,80},{112,96},{17,1},{33... | collective-permute-start | bytes 3080 | tf_op jit(solution)/shard_map/ppermute | solution.py:195
  6.9 2.9 %copy-start.2 = (s32[2,1]{0,1:T(1,128)S(1)}, s32[2,1]{0,1:T(1,128)}, u32[]{:S(2)}) copy-start(s32[2,1]{0,1:T(1,128)} %param.16) | copy-start | bytes 28
  6.9 33.4 %collective-permute-start.2 = (f32[4,128]{1,0:T(4,128)S(1)}, f32[4,128]{1,0:T(4,128)S(1)}, u32[]{:S(2)}, u32[]{:S(2)}) collective-permute-start(f32[4,128]{1,0:T(4,128)S(1)} %get-tuple-element.6), channel_id=1, source_target_pairs={{0,1},{1,2},{2,3},{3,4},{4,5},{5,6},{6,7},{7,8},{8,9},{9,10},{10,1... | collective-permute-start | bytes 6152 | tf_op jit(solution)/shard_map/ppermute | solution.py:194
  8.5 31.8 %collective-permute-start.3 = (f32[4,128]{1,0:T(4,128)S(1)}, f32[4,128]{1,0:T(4,128)S(1)}, u32[]{:S(2)}, u32[]{:S(2)}) collective-permute-start(f32[4,128]{1,0:T(4,128)S(1)} %get-tuple-element.7), channel_id=1, source_target_pairs={{1,0},{2,1},{3,2},{4,3},{5,4},{6,5},{7,6},{8,7},{9,8},{10,9},{11,1... | collective-permute-start | bytes 6152 | tf_op jit(solution)/shard_map/ppermute | solution.py:195
  39.3 0.9 copy-start
  114.5 22.6 %all-to-all-start = ((f32[16,128,128]{2,1,0:T(8,128)}), f32[16,128,128]{2,1,0:T(8,128)S(1)}, u32[]{:S(2)}, u32[]{:S(2)}) async-start(f32[16,128,128]{2,1,0:T(8,128)} %get-tuple-element.4), calls=%async_computation | async-start | bytes 2097152 | tf_op jit(solution)/shard_map/all_to_all | solution.py:200

commit v2 on v1

--- a/solution.py
+++ b/solution.py
@@ -23,9 +23,10 @@
     @pl.loop(0, blocks)
     def _(b):
         at = pl.multiple_of(b * 128, 128)
-        before = coarse_ref[:, pl.ds(at, 128)]
-        here = coarse_ref[:, pl.ds(at + 128, 128)]
-        after = coarse_ref[:, pl.ds(at + 256, 128)]
+        ahead = pl.multiple_of((b + blocks + 1) % (blocks + 2) * 128, 128)
+        before = coarse_ref[:, pl.ds(ahead, 128)]
+        here = coarse_ref[:, pl.ds(at, 128)]
+        after = coarse_ref[:, pl.ds(pl.multiple_of(at + 128, 128), 128)]
         low = jnp.concatenate([before[:, 64:], here[:, :64]], axis=1)
         high = jnp.concatenate([here[:, 64:], after[:, :64]], axis=1)
         for q, (window, shift) in enumerate(((low, 64), (here, 0), (here, 0), (high, -64))):
@@ -94,7 +95,15 @@
     ohot_ref[:, pl.ds(at + width, 128)] = hot
 
 
-def add_side(lhs_ref, ohot_ref, out_ref, period, at):
+def left_place(slot):
+    return slot % 2 * 8 + slot // 2 % 4 * 2 + slot // 8
+
+
+def right_place(slot):
+    return slot % 4 * 2 + slot // 4
+
+
+def add_side(lhs_ref, ohot_ref, out_ref, period, place, at):
     got = lax.dot_general(
         lhs_ref[...], ohot_ref[...], (((1,), (1,)), ((), ())), preferred_element_type=f32
     )
@@ -105,10 +114,10 @@
             for h in range(2):
                 row = (slot * groups + g) * 8
                 rows = pl.ds(pl.multiple_of(at + g * 16 + h * 8, 8), 8)
-                out_ref[slot, rows, :] += got[row : row + 8, h * 128 : h * 128 + 128]
-
-
-def add_own(fine_ref, out_ref, slot, period):
+                out_ref[place(slot), rows, :] += got[row : row + 8, h * 128 : h * 128 + 128]
+
+
+def add_own(fine_ref, out_ref, slot, period, place):
     group = pl.multiple_of((slot * period) // 8 * 8, 8)
     row = lax.broadcasted_iota(i32, (8, 128), 0)
     index = (slot * period) % 8 + row % period
@@ -121,7 +130,7 @@
             lanes = pl.ds(pl.multiple_of((block * spread + q) * 128, 128), 128)
             picked = jnp.take_along_axis(fine_ref[pl.ds(group, 8), lanes], index, axis=0)
             got = picked if got is None else jnp.where(row // period == q, picked, got)
-        out_ref[slot, pl.ds(pl.multiple_of(block * 8, 8), 8), :] += got
+        out_ref[place(slot), pl.ds(pl.multiple_of(block * 8, 8), 8), :] += got
 
 
 CHUNK = 512
@@ -160,11 +169,11 @@
             build_side([scaled * right[g] for g in range(4)], row, 2, lhs_ref.at[0], ohot_ref.at[0], at, CHUNK)
             build_side([scaled * left[g] for g in range(4)], col, 4, lhs_ref.at[1], ohot_ref.at[1], at, CHUNK)
 
-        add_side(lhs_ref.at[0], ohot_ref.at[0], ol_ref, 2, tile * 64)
-        add_side(lhs_ref.at[1], ohot_ref.at[1], or_ref, 4, 0)
-
-    add_own(fl_ref, ol_ref, my_col, 2)
-    add_own(fr_ref, or_ref, my_row, 4)
+        add_side(lhs_ref.at[0], ohot_ref.at[0], ol_ref, 2, left_place, tile * 64)
+        add_side(lhs_ref.at[1], ohot_ref.at[1], or_ref, 4, right_place, 0)
+
+    add_own(fl_ref, ol_ref, my_col, 2, left_place)
+    add_own(fr_ref, or_ref, my_row, 4, right_place)
 
 
 def local_step(mask, left, right, sl, wl, sr, wr, rows, cols, vals):
@@ -187,25 +196,207 @@
     )(mask, left, right, sl.reshape(1, -1), wl, sr.reshape(1, -1), wr, rows, cols, vals)
 
 
-def with_halo(block, axis):
-    count = lax.axis_size(axis)
-    forward = [(i, i + 1) for i in range(count - 1)]
-    backward = [(i + 1, i) for i in range(count - 1)]
-    low = lax.ppermute(block[:, -128:], axis, forward)
-    high = lax.ppermute(block[:, :128], axis, backward)
-    return jnp.concatenate([low, block, high], axis=1)
-
-
-def sum_at_owner(parts, axis):
-    return jnp.sum(lax.all_to_all(parts, axis, 0, 0, tiled=True), axis=0)
+MESH_ID = pl.DeviceIdType.MESH
+
+
+def greet(others):
+    barrier = pltpu.get_barrier_semaphore()
+    for other in others:
+        pl.semaphore_signal(barrier, inc=1, device_id=other, device_id_type=MESH_ID)
+    pl.semaphore_wait(barrier, len(others))
+
+
+def gather_kernel(
+    cl_ref, cr_ref, gl_ref, gr_ref, edge_send, edge_recv, main_send, main_recv, halo_send, halo_recv
+):
+    r = lax.axis_index("row")
+    c = lax.axis_index("col")
+    col_peers = [(r, (c + d) % 16) for d in range(1, 16)]
+    row_peers = [((r + d) % 8, c) for d in range(1, 8)]
+    greet(col_peers + row_peers)
+
+    def send(src, dst, sems, at, to):
+        copy = pltpu.make_async_remote_copy(
+            src_ref=src, dst_ref=dst, send_sem=sems[0].at[at], recv_sem=sems[1].at[at],
+            device_id=to, device_id_type=MESH_ID,
+        )
+        copy.start()
+        return copy
+
+    edges = (edge_send, edge_recv)
+    mains = (main_send, main_recv)
+    halos = (halo_send, halo_recv)
+    edge_copies = [
+        send(cl_ref.at[:, 0:128], gl_ref.at[c, :, 2048:2176], edges, 0, ((r + 7) % 8, c)),
+        send(cl_ref.at[:, 1920:2048], gl_ref.at[c, :, 2176:2304], edges, 1, ((r + 1) % 8, c)),
+        send(cr_ref.at[:, 0:128], gr_ref.at[r, :, 1024:1152], edges, 2, (r, (c + 15) % 16)),
+        send(cr_ref.at[:, 896:1024], gr_ref.at[r, :, 1152:1280], edges, 3, (r, (c + 1) % 16)),
+    ]
+    main_copies = [
+        send(cl_ref, gl_ref.at[c, :, 0:2048], mains, d, (r, (c + d) % 16)) for d in range(1, 16)
+    ] + [
+        send(cr_ref, gr_ref.at[r, :, 0:1024], mains, 15 + d, ((r + d) % 8, c)) for d in range(1, 8)
+    ]
+    gl_ref[c, :, 0:2048] = cl_ref[...]
+    gr_ref[r, :, 0:1024] = cr_ref[...]
+    for copy in edge_copies:
+        copy.wait()
+    halo_copies = [
+        send(gl_ref.at[c, :, 2048:2304], gl_ref.at[c, :, 2048:2304], halos, d, (r, (c + d) % 16))
+        for d in range(1, 16)
+    ] + [
+        send(gr_ref.at[r, :, 1024:1280], gr_ref.at[r, :, 1024:1280], halos, 15 + d, ((r + d) % 8, c))
+        for d in range(1, 8)
+    ]
+    for copy in main_copies:
+        copy.wait()
+    for copy in halo_copies:
+        copy.wait()
+
+    @pl.when(r == 0)
+    def _():
+        gl_ref[:, :, 2176:2304] = jnp.zeros((16, 2, 128), f32)
+
+    @pl.when(r == 7)
+    def _():
+        gl_ref[:, :, 2048:2176] = jnp.zeros((16, 2, 128), f32)
+
+    @pl.when(c == 0)
+    def _():
+        gr_ref[:, :, 1152:1280] = jnp.zeros((8, 4, 128), f32)
+
+    @pl.when(c == 15)
+    def _():
+        gr_ref[:, :, 1024:1152] = jnp.zeros((8, 4, 128), f32)
+
+
+def gather_coarse(coarse_left, coarse_right):
+    vmem = pl.BlockSpec(memory_space=pltpu.VMEM)
+    dma = pltpu.SemaphoreType.DMA
+    return pl.pallas_call(
+        gather_kernel,
+        out_shape=(
+            jax.ShapeDtypeStruct((16, 2, 2304), f32),
+            jax.ShapeDtypeStruct((8, 4, 1280), f32),
+        ),
+        in_specs=[vmem, vmem],
+        out_specs=(vmem, vmem),
+        scratch_shapes=[dma((4,)), dma((4,)), dma((23,)), dma((23,)), dma((23,)), dma((23,))],
+        compiler_params=pltpu.CompilerParams(collective_id=0, has_side_effects=True),
+        name="gather_coarse",
+    )(coarse_left, coarse_right)
+
+
+PIECES = 2
+
+
+def reduce_kernel(
+    gl_ref, gr_ref, ol_ref, or_ref,
+    pair_ref, sum_ref, ly_ref, lsum_ref, lz_ref, rx_ref, rsum_ref, rz_ref, sends, recvs,
+):
+    r = lax.axis_index("row")
+    c = lax.axis_index("col")
+    zlo, x = r // 4, r % 4
+    zhi, y, core = c // 8, (c // 2) % 4, c % 2
+    pair = (r, c + 1 - 2 * core)
+    y_peer = [(r, zhi * 8 + ((y + d) % 4) * 2 + core) for d in range(1, 4)]
+    x_peer = [(zlo * 4 + (x + d) % 4, c) for d in range(1, 4)]
+    left_z = (r, (c + 8) % 16)
+    right_z = ((r + 4) % 8, c)
+    greet([pair, left_z, right_z] + y_peer + x_peer)
+    rows = 128 // PIECES
+
+    def send(src, dst, at, to):
+        copy = pltpu.make_async_remote_copy(
+            src_ref=src, dst_ref=dst, send_sem=sends.at[at], recv_sem=recvs.at[at],
+            device_id=to, device_id_type=MESH_ID,
+        )
+        copy.start()
+        return copy
+
+    started = []
+    cut = [pl.ds(p * rows, rows) for p in range(PIECES)]
+    to_pair = [
+        send(gl_ref.at[pl.ds((1 - core) * 8, 8), cut[p]], pair_ref.at[:, cut[p]], p * 9, pair)
+        for p in range(PIECES)
+    ]
+    to_x = [
+        [
+            send(
+                gr_ref.at[pl.ds(((x + d) % 4) * 2, 2), cut[p]], rx_ref.at[d - 1, :, cut[p]],
+                p * 9 + d, x_peer[d - 1],
+            )
+            for d in range(1, 4)
+        ]
+        for p in range(PIECES)
+    ]
+    to_y = []
+    for p in range(PIECES):
+        to_pair[p].wait()
+        for s in range(8):
+            sum_ref[s, cut[p]] = gl_ref[core * 8 + s, cut[p]] + pair_ref[s, cut[p]]
+        to_y.append([
+            send(
+                sum_ref.at[pl.ds(((y + d) % 4) * 2, 2), cut[p]], ly_ref.at[d - 1, :, cut[p]],
+                p * 9 + 3 + d, y_peer[d - 1],
+            )
+            for d in range(1, 4)
+        ])
+    to_rz, to_lz = [], []
+    for p in range(PIECES):
+        for copy in to_x[p]:
+            copy.wait()
+        for s in range(2):
+            rsum_ref[s, cut[p]] = gr_ref[x * 2 + s, cut[p]] + (
+                rx_ref[0, s, cut[p]] + rx_ref[1, s, cut[p]] + rx_ref[2, s, cut[p]]
+            )
+        to_rz.append(send(rsum_ref.at[1 - zlo, cut[p]], rz_ref.at[cut[p]], p * 9 + 7, right_z))
+        for copy in to_y[p]:
+            copy.wait()
+        for s in range(2):
+            lsum_ref[s, cut[p]] = sum_ref[y * 2 + s, cut[p]] + (
+                ly_ref[0, s, cut[p]] + ly_ref[1, s, cut[p]] + ly_ref[2, s, cut[p]]
+            )
+        to_lz.append(send(lsum_ref.at[1 - zhi, cut[p]], lz_ref.at[cut[p]], p * 9 + 8, left_z))
+    for p in range(PIECES):
+        to_rz[p].wait()
+        or_ref[cut[p]] = rsum_ref[zlo, cut[p]] + rz_ref[cut[p]]
+        to_lz[p].wait()
+        ol_ref[cut[p]] = lsum_ref[zhi, cut[p]] + lz_ref[cut[p]]
+
+
+def reduce_grads(gl, gr):
+    vmem = pl.BlockSpec(memory_space=pltpu.VMEM)
+    dma = pltpu.SemaphoreType.DMA
+    block = (128, 128)
+    return pl.pallas_call(
+        reduce_kernel,
+        out_shape=(jax.ShapeDtypeStruct(block, f32), jax.ShapeDtypeStruct(block, f32)),
+        in_specs=[vmem, vmem],
+        out_specs=(vmem, vmem),
+        scratch_shapes=[
+            pltpu.VMEM((8, *block), f32),
+            pltpu.VMEM((8, *block), f32),
+            pltpu.VMEM((3, 2, *block), f32),
+            pltpu.VMEM((2, *block), f32),
+            pltpu.VMEM(block, f32),
+            pltpu.VMEM((3, 2, *block), f32),
+            pltpu.VMEM((2, *block), f32),
+            pltpu.VMEM(block, f32),
+            dma((9 * PIECES,)),
+            dma((9 * PIECES,)),
+        ],
+        compiler_params=pltpu.CompilerParams(collective_id=1, has_side_effects=True),
+        name="reduce_grads",
+    )(gl, gr)
 
 
 def on_device(coarse_left, coarse_right, sl, wl, sr, wr, mask, rows, cols, vals):
-    left = lax.all_gather(with_halo(coarse_left, "row"), "col", axis=0, tiled=True)
-    right = lax.all_gather(with_halo(coarse_right, "col"), "row", axis=0, tiled=True)
-    gl, gr = local_step(mask, left, right, sl, wl, sr, wr, rows, cols, vals)
-    left_new = sum_at_owner(gl, "col").reshape(64, 2, 128).transpose(1, 0, 2).reshape(2, 8192)
-    right_new = sum_at_owner(gr, "row").reshape(32, 4, 128).transpose(1, 0, 2).reshape(4, 4096)
+    left, right = gather_coarse(coarse_left, coarse_right)
+    gl, gr = local_step(mask, left.reshape(32, 2304), right.reshape(32, 1280), sl, wl, sr, wr, rows, cols, vals)
+    left_sum, right_sum = reduce_grads(gl, gr)
+    left_new = left_sum.reshape(64, 2, 128).transpose(1, 0, 2).reshape(2, 8192)
+    right_new = right_sum.reshape(32, 4, 128).transpose(1, 0, 2).reshape(4, 4096)
     return left_new, right_new
 
 

time: 139 us -> 74.7 us (0.54)
  blocking collectives: 71.5 us -> 0 us
  Pallas kernels: 30.9 us -> 67.7 us
  waiting for transfers between devices: 17.3 us -> 0 us
  starting transfers between devices: 12.3 us -> 0 us
  local copies, waits for them, and re-layouts: 3.73 us -> 6.05 us
    all_gather x2 -> x0, blocking collectives: 58.2 us -> none  [the longest x1 29.3 us: on_device(): lax.all_gather(with_halo(coarse_right, 'col'), 'row', axis=0, tiled=True)]
    pallas_call x0 -> x2, Pallas kernels: none -> 36.5 us  [the longest x1 18.7 us: reduce_grads(): pl.pallas_call(reduce_kernel, out_shape=(jax.ShapeDtypeStruct(block, f32)...]
    all_to_all x1 -> x0, waiting for transfers between devices: 17.3 us -> none  [sum_at_owner(): return jnp.sum(lax.all_to_all(parts, axis, 0, 0, tiled=True), axis=0)]
    all_to_all x1 -> x0, blocking collectives: 13.3 us -> none  [sum_at_owner(): return jnp.sum(lax.all_to_all(parts, axis, 0, 0, tiled=True), axis=0)]
    ppermute x4 -> x0, starting transfers between devices: 7.66 us -> none  [the longest x2 5.07 us: with_halo(): low = lax.ppermute(block[:, -128:], axis, forward)]
    all_to_all x1 -> x0, starting transfers between devices: 4.61 us -> none  [sum_at_owner(): return jnp.sum(lax.all_to_all(parts, axis, 0, 0, tiled=True), axis=0)]
    reshape x0 -> x2, local copies, waits for them, and re-layouts: none -> 2.61 us  [the longest x1 1.9 us: on_device(): left.reshape(32, 2304)]
    slice x2 -> x0, local copies, waits for them, and re-layouts: 1.45 us -> none  [with_halo(): low = lax.ppermute(block[:, -128:], axis, forward)]
  transfers between devices with their start and end apart: 5 -> 0, of which waited for: 1 -> 0; matrix products, arithmetic and copies ran while one was open for 2% -> 0% of each run, Pallas kernels for 0% -> 0%
where the time goes in v2:
time: 74.7 us; the launch traced here: 74.4 us
  Pallas kernels  67.7 us (91%)
  local copies, waits for them, and re-layouts  6.05 us (8%)
    pallas_call x1, Pallas kernels, local_step(): pl.pallas_call(local_kernel, out_shape=(jax.ShapeDtypeStruct((16, 128, 12...  31.2 us
    pallas_call x1, Pallas kernels, reduce_grads(): pl.pallas_call(reduce_kernel, out_shape=(jax.ShapeDtypeStruct(block, f32)...  18.7 us
    pallas_call x1, Pallas kernels, gather_coarse(): pl.pallas_call(gather_kernel, out_shape=(jax.ShapeDtypeStruct((16, 2, 230...  17.9 us
    unnamed x9, local copies, waits for them, and re-layouts  3.44 us
    reshape x1, local copies, waits for them, and re-layouts, on_device(): left.reshape(32, 2304)  1.9 us

profile of v2, /device:TPU:0, one launch (start us, length us, event | category | flops | bytes accessed | tf_op | source)
XLA Modules:
  0.0 74.4 jit_solution(11741846324770184579)
XLA Ops:
  0.6 0.0 copy-start.2
  0.6 0.6 copy-done.2
  1.3 0.6 copy.12.mask_ref
  1.9 17.9 %gather_coarse.1 = (f32[16,2,2304]{2,1,0:T(2,128)}, f32[8,4,1280]{2,1,0:T(4,128)}) custom-call(f32[2,2048]{1,0:T(2,128)} %cl_ref.1, f32[4,1024]{1,0:T(4,128)} %cr_ref.1), custom_call_target="tpu_custom_call" | custom-call | tf_op jit(solution)/shard_map/gather_coarse/pallas_call | solution.py:276
  19.8 0.0 copy-start
  19.8 1.9 %reshape.28.left_ref = f32[32,2304]{1,0:T(8,128)} reshape(f32[16,2,2304]{2,1,0:T(2,128)} %get-tuple-element.8) | data formatting | bytes 589824 | tf_op jit(solution)/shard_map/reshape | solution.py:396
  21.7 0.0 copy-done
  21.7 0.7 reshape.29.right_ref
  22.4 31.2 %local_step.1 = (f32[16,128,128]{2,1,0:T(8,128)}, f32[8,128,128]{2,1,0:T(8,128)}) custom-call(s32[2,1]{1,0:T(2,128)} %copy.12.mask_ref, f32[32,2304]{1,0:T(8,128)} %reshape.28.left_ref, f32[32,1280]{1,0:T(8,128)} %reshape.29.right_ref, s32[1,8192]{1,0:T(1,128)} %bitcast.14, f32[4,8192]{1,0:T(4,128)} %wl_ref.1, s32[1,4096]{1,0:T(1,128)} %bitcast.15, ...), custom_call_target="tpu_custom_call" | custom-call | tf_op jit(solution)/shard_map/local_step/pallas_call | solution.py:181
  53.6 18.7 %reduce_grads.1 = (f32[128,128]{1,0:T(8,128)}, f32[128,128]{1,0:T(8,128)}) custom-call(f32[16,128,128]{2,1,0:T(8,128)} %get-tuple-element.10.gl_ref, f32[8,128,128]{2,1,0:T(8,128)} %get-tuple-element.11.gr_ref), custom_call_target="tpu_custom_call" | custom-call | tf_op jit(solution)/shard_map/reduce_grads/pallas_call | solution.py:372
  72.3 0.0 copy-start.1
  72.3 1.5 %copy.17 = f32[2,8192]{1,0:T(2,128)} copy(f32[2,8192]{1,0:T(2,128)} %bitcast.13) | data formatting | bytes 131072
  73.8 0.0 copy-done.1
  73.8 0.6 copy.18
Async XLA Ops:
  0.6 0.7 copy-start.2
  19.8 1.9 %copy-start = (f32[8,4,1280]{2,1,0:T(4,128)S(1)}, f32[8,4,1280]{2,1,0:T(4,128)}, u32[]{:S(2)}) copy-start(f32[8,4,1280]{2,1,0:T(4,128)} %get-tuple-element.9) | copy-start | bytes 491524
  72.3 1.5 %copy-start.1 = (f32[128,128]{1,0:T(8,128)S(1)}, f32[128,128]{1,0:T(8,128)}, u32[]{:S(2)}) copy-start(f32[128,128]{1,0:T(8,128)} %get-tuple-element.13) | copy-start | bytes 196612

commit v3 on v2

v3 whole, which is shorter than its diff:
```python
import functools
import jax, jax.numpy as jnp
from jax import lax
from jax.sharding import PartitionSpec as P
from jax.experimental import pallas as pl
from jax.experimental.pallas import tpu as pltpu

TILE = 4096
SPT = 2048
BLOCK = 512
BLOCKS = 2 * SPT // BLOCK
PER_TILE = SPT // BLOCK
ETA = 0.5
f32, bf16, i32 = jnp.float32, jnp.bfloat16, jnp.int32


def lanes(at, size=128):
    return pl.ds(pl.multiple_of(at, 128), size)


def lane_pick(table, index):
    return jnp.take_along_axis(table, index, axis=1)


LEFT_STEPS, RIGHT_STEPS = 17, 9
PAD = 384


def upsample_matrix(up_ref):
    row = lax.broadcasted_iota(i32, (16, 128), 0)
    lane = lax.broadcasted_iota(i32, (16, 128), 1)
    for pattern in range(2):
        for offset in range(6):
            gap = (32 * pattern + 30 + offset + (lane >> 2) - row).astype(f32).astype(bf16)
            one, zero = jnp.ones((16, 128), bf16), jnp.zeros((16, 128), bf16)
            for m in range(8):
                part = jnp.where(gap == jnp.full((16, 128), 16 * m, bf16), one, zero)
                at = (pattern * 6 + offset) * 128
                up_ref[16 * m : 16 * m + 16, at : at + 128] = part
                up_ref[128 + 16 * m : 144 + 16 * m, at : at + 128] = part


def spread_weights(stencil_ref, weight_ref, by_offset_ref, origin, count):
    row = lax.broadcasted_iota(i32, (8, 128), 0)
    lane = lax.broadcasted_iota(i32, (8, 128), 1)

    def step(block, _):
        weight = jnp.concatenate(
            [weight_ref[:, lanes(block * 128)], jnp.zeros((4, 128), f32)], axis=0
        )
        stencil = jnp.broadcast_to(stencil_ref[:, lanes(block * 128)], (8, 128))
        base = stencil - (origin + block * 32) - (lane >> 2)
        by_offset_ref[:, lanes(block * 128 + PAD)] = jnp.take_along_axis(
            weight, (row - 1 - base) & 7, axis=0
        )
        return 0

    lax.fori_loop(0, count // 128, step, 0, unroll=4)


def two_terms(value):
    top = value.astype(bf16)
    return top, (value - top.astype(f32)).astype(bf16)


def coarse_windows(coarse, lhs_ref, base, steps):
    def step(b, _):
        here = coarse((b + steps) % (steps + 1))
        after = coarse(b)
        mid = jnp.concatenate([here[:, 64:], after[:, :64]], axis=1)
        for w, window in enumerate((here, mid)):
            top, rest = two_terms(window)
            rows = pl.ds(pl.multiple_of(base + b * 64 + w * 32, 32), 32)
            lhs_ref[rows, 0:128] = top
            lhs_ref[rows, 128:256] = rest
        return 0

    lax.fori_loop(0, steps, step, 0)


def interpolate(lhs_ref, up_ref, by_offset_ref, fine_ref, base, steps):
    for tile in range(6):
        pattern, first = tile // 3, tile % 3 * 2
        got = jnp.dot(
            lhs_ref[base : base + steps * 64, :],
            up_ref[:, tile * 256 : tile * 256 + 256],
            preferred_element_type=f32,
        )
        for b in range(steps):
            for w in range(2):
                at = slice(b * 512 + (2 * w + pattern) * 128, b * 512 + (2 * w + pattern) * 128 + 128)
                weight = [
                    jnp.broadcast_to(by_offset_ref[first + n : first + n + 1, at], (8, 128))
                    for n in range(2)
                ]
                for g in range(4):
                    row = b * 64 + w * 32 + g * 8
                    part = got[row : row + 8, 0:128] * weight[0] + got[row : row + 8, 128:256] * weight[1]
                    if first:
                        part = part + fine_ref[8 * g : 8 * g + 8, at]
                    fine_ref[8 * g : 8 * g + 8, at] = part


def pick_columns(fine_ref, start, position):
    j = jnp.broadcast_to(position >> 7, (8, 128))
    lo = jnp.broadcast_to(position & 127, (8, 128))
    bits = [(j & (1 << b)) != 0 for b in range(5)]

    def tree(g, prefix, bit):
        if bit < 0:
            return lane_pick(fine_ref[8 * g : 8 * g + 8, lanes(PAD + start + prefix * 128)], lo)
        off = tree(g, prefix, bit - 1)
        on = tree(g, prefix | 1 << bit, bit - 1)
        return jnp.where(bits[bit], on, off)

    return [tree(g, 0, 4) for g in range(4)]


def build_table(fine_ref, table_ref):
    def step(hi, _):
        for h in range(2):
            j = (hi >> 1) * 4 + h * 2 + (hi & 1)
            for half in range(2):
                v = fine_ref[16 * half : 16 * half + 16, lanes(PAD + j * 128)]
                top, rest = two_terms(v)
                rows = pl.ds(pl.multiple_of(hi * 32 + 16 * half, 16), 16)
                table_ref[rows, h * 128 : h * 128 + 128] = top
                table_ref[rows, 256 + h * 128 : 384 + h * 128] = rest
        return 0

    lax.fori_loop(0, 16, step, 0, unroll=4)


def one_hot(lo):
    lo16 = jnp.broadcast_to(lo, (16, 128)) - lax.broadcasted_iota(i32, (16, 128), 0)
    lo16 = lo16.astype(f32).astype(bf16)
    one, zero = jnp.ones((16, 128), bf16), jnp.zeros((16, 128), bf16)
    return jnp.concatenate(
        [jnp.where(lo16 == jnp.full((16, 128), 16 * m, bf16), one, zero) for m in range(16)], axis=0
    )


def table_columns(table_ref, positions):
    split = [split_position(p, 4) for p in positions]
    hot = jnp.concatenate([one_hot(lo) for _, lo in split], axis=1)
    rhs = jnp.concatenate([hot, hot], axis=0)
    got = jnp.dot(table_ref[...], rhs, preferred_element_type=f32)
    out = []
    for sub, (hi, _) in enumerate(split):
        hi8 = jnp.broadcast_to(hi, (8, 128))
        bits = [(hi8 & (1 << b)) != 0 for b in range(4)]

        def tree(g, prefix, bit):
            if bit < 0:
                row = prefix * 32 + 8 * g
                return got[row : row + 8, sub * 128 : sub * 128 + 128]
            return jnp.where(bits[bit], tree(g, prefix | 1 << bit, bit - 1), tree(g, prefix, bit - 1))

        out.append([tree(g, 0, 3) for g in range(4)])
    return out


def sample_block(blk, fl_ref, table_ref, vl_ref, vr_ref, rows_ref, cols_ref, vals_ref, mask_ref):
    tile = blk // PER_TILE
    subs = [(blk % PER_TILE) * BLOCK + sub * 128 for sub in range(BLOCK // 128)]
    rights = table_columns(table_ref, [cols_ref[tile, :, lanes(at)] for at in subs])
    keep = mask_ref[0, tile].astype(f32) * -ETA
    for sub, at in enumerate(subs):
        left = pick_columns(fl_ref, tile * TILE, rows_ref[tile, :, lanes(at)])
        right = rights[sub]
        dots = (left[0] * right[0] + left[1] * right[1]) + (left[2] * right[2] + left[3] * right[3])
        error = jnp.sum(dots, axis=0, keepdims=True) - vals_ref[tile, :, lanes(at)]
        scaled = jnp.broadcast_to(error * keep, (8, 128))
        out = lanes(blk * BLOCK + sub * 128)
        for g in range(4):
            vl_ref[8 * g : 8 * g + 8, out] = scaled * right[g]
            vr_ref[8 * g : 8 * g + 8, out] = scaled * left[g]


def split_position(position, period):
    half = 8 // period
    j = position >> 7
    hi = (j // (2 * half)) * half + (j & (half - 1))
    lo = ((j // half) & 1) * 128 + (position & 127)
    return hi, lo


def scatter_block(blk, value_ref, position_ref, out_ref, period, place, at):
    tile = blk // PER_TILE
    per_tile = 16 // period
    count = 16 // per_tile
    row16 = lax.broadcasted_iota(i32, (16, 128), 0)
    hots, tops, rests = [], [], []
    for sub in range(BLOCK // 128):
        position = position_ref[tile, :, lanes((blk % PER_TILE) * BLOCK + sub * 128)]
        hi, lo = split_position(position, period)
        hi16 = jnp.broadcast_to(hi, (16, 128)) - row16 // period
        masks = [jnp.where(hi16 == m * per_tile, 1.0, 0.0).astype(bf16) for m in range(count)]
        hots.append(one_hot(lo))
        top_rows, rest_rows = [], []
        for g in range(4):
            v = value_ref[8 * g : 8 * g + 8, lanes(blk * BLOCK + sub * 128)]
            for first in range(0, 8, period):
                index = first + lax.broadcasted_iota(i32, (8, 128), 0) % period
                dup = jnp.take_along_axis(v, index, axis=0)
                dup = jnp.concatenate([dup, dup], axis=0)
                top, rest = two_terms(dup)
                for mask in masks:
                    top_rows.append(top * mask)
                    rest_rows.append(rest * mask)
        tops.append(top_rows)
        rests.append(rest_rows)
    pieces = [jnp.concatenate(p, axis=0) for p in tops + rests]
    lhs = jnp.concatenate(pieces, axis=1)
    rhs = jnp.concatenate(hots + hots, axis=1)
    got = lax.dot_general(lhs, rhs, (((1,), (1,)), ((), ())), preferred_element_type=f32)
    slots = 32 // period
    groups = 64 // slots
    for slot in range(slots):
        for g in range(groups):
            for h in range(2):
                row = (slot * groups + g) * 8
                rows = pl.ds(pl.multiple_of(at + g * 16 + h * 8, 8), 8)
                out_ref[place(slot), rows, :] += got[row : row + 8, h * 128 : h * 128 + 128]


def left_place(slot):
    return slot % 2 * 8 + slot // 2 % 4 * 2 + slot // 8


def right_place(slot):
    return slot % 4 * 2 + slot // 4


def add_own(fine_ref, out_ref, slot, period, place):
    group = pl.multiple_of((slot * period) // 8 * 8, 8)
    row = lax.broadcasted_iota(i32, (8, 128), 0)
    index = (slot * period) % 8 + row % period
    spread = 8 // period

    def step(block, _):
        got = None
        for q in range(spread):
            tall = fine_ref[pl.ds(group, 8), lanes(PAD + (block * spread + q) * 128)]
            picked = jnp.take_along_axis(tall, index, axis=0)
            got = picked if got is None else jnp.where(row // period == q, picked, got)
        out_ref[place(slot), pl.ds(pl.multiple_of(block * 8, 8), 8), :] = got
        return 0

    lax.fori_loop(0, 16, step, 0, unroll=4)


MESH_ID = pl.DeviceIdType.MESH


def greet(others):
    barrier = pltpu.get_barrier_semaphore()
    for other in others:
        pl.semaphore_signal(barrier, inc=1, device_id=other, device_id_type=MESH_ID)
    pl.semaphore_wait(barrier, len(others))


def gather_coarse(
    r, c, cl_ref, cr_ref, gl_ref, gr_ref, edge_send, edge_recv, main_send, main_recv, halo_send, halo_recv
):
    def send(src, dst, sems, at, to):
        copy = pltpu.make_async_remote_copy(
            src_ref=src, dst_ref=dst, send_sem=sems[0].at[at], recv_sem=sems[1].at[at],
            device_id=to, device_id_type=MESH_ID,
        )
        copy.start()
        return copy

    edges = (edge_send, edge_recv)
    mains = (main_send, main_recv)
    halos = (halo_send, halo_recv)
    edge_copies = [
        send(cl_ref.at[:, 0:128], gl_ref.at[c, :, 2048:2176], edges, 0, ((r + 7) % 8, c)),
        send(cl_ref.at[:, 1920:2048], gl_ref.at[c, :, 2176:2304], edges, 1, ((r + 1) % 8, c)),
        send(cr_ref.at[:, 0:128], gr_ref.at[r, :, 1024:1152], edges, 2, (r, (c + 15) % 16)),
        send(cr_ref.at[:, 896:1024], gr_ref.at[r, :, 1152:1280], edges, 3, (r, (c + 1) % 16)),
    ]
    main_copies = [
        send(cl_ref, gl_ref.at[c, :, 0:2048], mains, d, (r, (c + d) % 16)) for d in range(1, 16)
    ] + [
        send(cr_ref, gr_ref.at[r, :, 0:1024], mains, 15 + d, ((r + d) % 8, c)) for d in range(1, 8)
    ]
    gl_ref[c, :, 0:2048] = cl_ref[...]
    gr_ref[r, :, 0:1024] = cr_ref[...]
    for copy in edge_copies:
        copy.wait()
    halo_copies = [
        send(gl_ref.at[c, :, 2048:2304], gl_ref.at[c, :, 2048:2304], halos, d, (r, (c + d) % 16))
        for d in range(1, 16)
    ] + [
        send(gr_ref.at[r, :, 1024:1280], gr_ref.at[r, :, 1024:1280], halos, 15 + d, ((r + d) % 8, c))
        for d in range(1, 8)
    ]
    for copy in main_copies:
        copy.wait()
    for copy in halo_copies:
        copy.wait()

    @pl.when(r == 0)
    def _():
        gl_ref[:, :, 2176:2304] = jnp.zeros((16, 2, 128), f32)

    @pl.when(r == 7)
    def _():
        gl_ref[:, :, 2048:2176] = jnp.zeros((16, 2, 128), f32)

    @pl.when(c == 0)
    def _():
        gr_ref[:, :, 1152:1280] = jnp.zeros((8, 4, 128), f32)

    @pl.when(c == 15)
    def _():
        gr_ref[:, :, 1024:1152] = jnp.zeros((8, 4, 128), f32)


PIECES = 2


def reduce_grads(
    r, c, gl_ref, gr_ref, ol_ref, or_ref,
    pair_ref, sum_ref, ly_ref, lsum_ref, lz_ref, rx_ref, rsum_ref, rz_ref, sends, recvs,
):
    zlo, x = r // 4, r % 4
    zhi, y, core = c // 8, (c // 2) % 4, c % 2
    pair = (r, c + 1 - 2 * core)
    y_peer = [(r, zhi * 8 + ((y + d) % 4) * 2 + core) for d in range(1, 4)]
    x_peer = [(zlo * 4 + (x + d) % 4, c) for d in range(1, 4)]
    left_z = (r, (c + 8) % 16)
    right_z = ((r + 4) % 8, c)
    rows = 128 // PIECES

    def send(src, dst, at, to):
        copy = pltpu.make_async_remote_copy(
            src_ref=src, dst_ref=dst, send_sem=sends.at[at], recv_sem=recvs.at[at],
            device_id=to, device_id_type=MESH_ID,
        )
        copy.start()
        return copy

    cut = [pl.ds(p * rows, rows) for p in range(PIECES)]
    to_pair = [
        send(gl_ref.at[pl.ds((1 - core) * 8, 8), cut[p]], pair_ref.at[:, cut[p]], p * 9, pair)
        for p in range(PIECES)
    ]
    to_x = [
        [
            send(
                gr_ref.at[pl.ds(((x + d) % 4) * 2, 2), cut[p]], rx_ref.at[d - 1, :, cut[p]],
                p * 9 + d, x_peer[d - 1],
            )
            for d in range(1, 4)
        ]
        for p in range(PIECES)
    ]
    to_y = []
    for p in range(PIECES):
        to_pair[p].wait()
        for s in range(8):
            sum_ref[s, cut[p]] = gl_ref[core * 8 + s, cut[p]] + pair_ref[s, cut[p]]
        to_y.append([
            send(
                sum_ref.at[pl.ds(((y + d) % 4) * 2, 2), cut[p]], ly_ref.at[d - 1, :, cut[p]],
                p * 9 + 3 + d, y_peer[d - 1],
            )
            for d in range(1, 4)
        ])
    to_rz, to_lz = [], []
    for p in range(PIECES):
        for copy in to_x[p]:
            copy.wait()
        for s in range(2):
            rsum_ref[s, cut[p]] = gr_ref[x * 2 + s, cut[p]] + (
                rx_ref[0, s, cut[p]] + rx_ref[1, s, cut[p]] + rx_ref[2, s, cut[p]]
            )
        to_rz.append(send(rsum_ref.at[1 - zlo, cut[p]], rz_ref.at[cut[p]], p * 9 + 7, right_z))
        for copy in to_y[p]:
            copy.wait()
        for s in range(2):
            lsum_ref[s, cut[p]] = sum_ref[y * 2 + s, cut[p]] + (
                ly_ref[0, s, cut[p]] + ly_ref[1, s, cut[p]] + ly_ref[2, s, cut[p]]
            )
        to_lz.append(send(lsum_ref.at[1 - zhi, cut[p]], lz_ref.at[cut[p]], p * 9 + 8, left_z))
    for p in range(PIECES):
        to_rz[p].wait()
        or_ref[cut[p]] = rsum_ref[zlo, cut[p]] + rz_ref[cut[p]]
        to_lz[p].wait()
        ol_ref[cut[p]] = lsum_ref[zhi, cut[p]] + lz_ref[cut[p]]


def step_kernel(
    mask_ref, cl_ref, cr_ref, sl_ref, wl_ref, sr_ref, wr_ref, rows_ref, cols_ref, vals_ref,
    ol_ref, or_ref,
    gl_ref, gr_ref, fl_ref, fr_ref, wl6_ref, wr6_ref, vl_ref, vr_ref, pl_ref, pr_ref,
    pair_ref, sum_ref, ly_ref, lsum_ref, lz_ref, rx_ref, rsum_ref, rz_ref,
    edge_send, edge_recv, main_send, main_recv, halo_send, halo_recv, sends, recvs,
):
    r = lax.axis_index("row")
    c = lax.axis_index("col")
    greet([(r, (c + d) % 16) for d in range(1, 16)] + [((r + d) % 8, c) for d in range(1, 8)])
    gather_coarse(
        r, c, cl_ref, cr_ref, gl_ref, gr_ref, edge_send, edge_recv, main_send, main_recv, halo_send, halo_recv
    )
    spread_weights(sl_ref, wl_ref, wl6_ref, r * 2048, 8192)
    spread_weights(sr_ref, wr_ref, wr6_ref, c * 1024, 4096)

    def local(up_ref, lhs_ref, table_ref):
        upsample_matrix(up_ref)
        coarse_windows(lambda b: gl_ref[:, :, lanes(b * 128)].reshape(32, 128), lhs_ref, 0, LEFT_STEPS)
        coarse_windows(
            lambda b: gr_ref[:, :, lanes(b * 128)].reshape(32, 128), lhs_ref, LEFT_STEPS * 64, RIGHT_STEPS
        )
        interpolate(lhs_ref, up_ref, wl6_ref, fl_ref, 0, LEFT_STEPS)
        interpolate(lhs_ref, up_ref, wr6_ref, fr_ref, LEFT_STEPS * 64, RIGHT_STEPS)
        pl_ref[...] = jnp.zeros(pl_ref.shape, f32)
        pr_ref[...] = jnp.zeros(pr_ref.shape, f32)
        add_own(fl_ref, pl_ref, c, 2, left_place)
        add_own(fr_ref, pr_ref, r, 4, right_place)
        build_table(fr_ref, table_ref)

        def sample(blk):
            sample_block(blk, fl_ref, table_ref, vl_ref, vr_ref, rows_ref, cols_ref, vals_ref, mask_ref)

        def scatter(blk):
            scatter_block(blk, vl_ref, rows_ref, pl_ref, 2, left_place, blk // PER_TILE * 64)
            scatter_block(blk, vr_ref, cols_ref, pr_ref, 4, right_place, 0)

        sample(0)

        @pl.loop(1, BLOCKS)
        def _(blk):
            scatter(blk - 1)
            sample(blk)

        scatter(BLOCKS - 1)

    pl.run_scoped(
        local,
        pltpu.VMEM((256, 1536), bf16),
        pltpu.VMEM(((LEFT_STEPS + RIGHT_STEPS) * 64, 256), bf16),
        pltpu.VMEM((512, 512), bf16),
    )
    reduce_grads(
        r, c, pl_ref, pr_ref, ol_ref, or_ref,
        pair_ref, sum_ref, ly_ref, lsum_ref, lz_ref, rx_ref, rsum_ref, rz_ref, sends, recvs,
    )


def on_device(coarse_left, coarse_right, sl, wl, sr, wr, mask, rows, cols, vals):
    vmem = pl.BlockSpec(memory_space=pltpu.VMEM)
    smem = pl.BlockSpec(memory_space=pltpu.SMEM)
    dma = pltpu.SemaphoreType.DMA
    block = (128, 128)
    left_sum, right_sum = pl.pallas_call(
        step_kernel,
        out_shape=(jax.ShapeDtypeStruct(block, f32), jax.ShapeDtypeStruct(block, f32)),
        in_specs=[smem] + [vmem] * 9,
        out_specs=(vmem, vmem),
        scratch_shapes=[
            pltpu.VMEM((16, 2, 2304), f32),
            pltpu.VMEM((8, 4, 1280), f32),
            pltpu.VMEM((32, 512 * LEFT_STEPS), f32),
            pltpu.VMEM((32, 512 * RIGHT_STEPS), f32),
            pltpu.VMEM((8, 512 * LEFT_STEPS), f32),
            pltpu.VMEM((8, 512 * RIGHT_STEPS), f32),
            pltpu.VMEM((32, 2 * SPT), f32),
            pltpu.VMEM((32, 2 * SPT), f32),
            pltpu.VMEM((16, *block), f32),
            pltpu.VMEM((8, *block), f32),
            pltpu.VMEM((8, *block), f32),
            pltpu.VMEM((8, *block), f32),
            pltpu.VMEM((3, 2, *block), f32),
            pltpu.VMEM((2, *block), f32),
            pltpu.VMEM(block, f32),
            pltpu.VMEM((3, 2, *block), f32),
            pltpu.VMEM((2, *block), f32),
            pltpu.VMEM(block, f32),
            dma((4,)), dma((4,)), dma((23,)), dma((23,)), dma((23,)), dma((23,)),
            dma((9 * PIECES,)), dma((9 * PIECES,)),
        ],
        compiler_params=pltpu.CompilerParams(collective_id=0, has_side_effects=True),
        name="fused_step",
    )(
        mask.reshape(1, 2), coarse_left, coarse_right, sl.reshape(1, -1), wl, sr.reshape(1, -1), wr,
        rows, cols, vals,
    )
    left_new = left_sum.reshape(64, 2, 128).transpose(1, 0, 2).reshape(2, 8192)
    right_new = right_sum.reshape(32, 4, 128).transpose(1, 0, 2).reshape(4, 4096)
    return left_new, right_new


def solution(mesh):
    in_specs = (
        P("col", "row"),
        P("row", "col"),
        P("row"),
        P(None, "row"),
        P("col"),
        P(None, "col"),
        P("row", "col"),
        P("row", "col", None),
        P("row", "col", None),
        P("row", "col", None),
    )
    out_specs = (P("col", "row"), P("row", "col"))
    return jax.shard_map(
        on_device, mesh=mesh, in_specs=in_specs, out_specs=out_specs, check_vma=False
    )
```

time: 74.7 us -> 50.2 us (0.67)
  Pallas kernels: 67.7 us -> 47.3 us
  local copies, waits for them, and re-layouts: 6.05 us -> 2.14 us
    pallas_call x3 -> x1, Pallas kernels: 67.7 us -> 47.3 us  [on_device(): pl.pallas_call(step_kernel, out_shape=(jax.ShapeDtypeStruct(block, f32),...]
    reshape x2 -> x0, local copies, waits for them, and re-layouts: 2.61 us -> none  [the longest x1 1.9 us: on_device(): left.reshape(32, 2304)]
    unnamed x9 -> x4, local copies, waits for them, and re-layouts: 3.44 us -> 2.14 us
where the time goes in v3:
time: 50.2 us; the launch traced here: 50.1 us
  Pallas kernels  47.3 us (94%)
  local copies, waits for them, and re-layouts  2.14 us (4%)
  between operations  0.65 us (1%)
    pallas_call x1, Pallas kernels, on_device(): pl.pallas_call(step_kernel, out_shape=(jax.ShapeDtypeStruct(block, f32),...  47.3 us
    unnamed x4, local copies, waits for them, and re-layouts  2.14 us

profile of v3, /device:TPU:0, one launch (start us, length us, event | category | flops | bytes accessed | tf_op | source)
XLA Modules:
  0.0 50.1 jit_solution(18381511394245284052)
XLA Ops:
  0.6 47.3 %fused_step.1 = (f32[128,128]{1,0:T(8,128)}, f32[128,128]{1,0:T(8,128)}) custom-call(s32[1,2]{1,0:T(1,128)} %bitcast.17, f32[2,2048]{1,0:T(2,128)} %cl_ref.1, f32[4,1024]{1,0:T(4,128)} %cr_ref.1, s32[1,8192]{1,0:T(1,128)} %bitcast.15, f32[4,8192]{1,0:T(4,128)} %wl_ref.1, s32[1,4096]{1,0:T(1,128)} %bitcast.16, f32[4,4096]{1,0:T(4,128)} %wr_ref.1, ...), custom_call_target="tpu_custom_call" | custom-call | tf_op jit(solution)/shard_map/fused_step/pallas_call | solution.py:458
  47.9 0.0 copy-start
  47.9 1.5 %copy.16 = f32[2,8192]{1,0:T(2,128)} copy(f32[2,8192]{1,0:T(2,128)} %bitcast.14) | data formatting | bytes 131072
  49.4 0.0 copy-done
  49.4 0.6 %copy.17 = f32[4,4096]{1,0:T(4,128)} copy(f32[4,4096]{1,0:T(4,128)S(1)} %bitcast.13) | data formatting | bytes 131072
Async XLA Ops:
  47.9 1.5 %copy-start = (f32[128,128]{1,0:T(8,128)S(1)}, f32[128,128]{1,0:T(8,128)}, u32[]{:S(2)}) copy-start(f32[128,128]{1,0:T(8,128)} %get-tuple-element.5) | copy-start | bytes 196612

commit v4 on v3

v4 whole, which is shorter than its diff:
```python
import functools
import jax, jax.numpy as jnp
from jax import lax
from jax.sharding import PartitionSpec as P
from jax.experimental import pallas as pl
from jax.experimental.pallas import tpu as pltpu

TILE = 4096
SPT = 2048
BLOCK = 512
BLOCKS = 2 * SPT // BLOCK
PER_TILE = SPT // BLOCK
ETA = 0.5
f32, bf16, i32 = jnp.float32, jnp.bfloat16, jnp.int32


def lanes(at, size=128):
    return pl.ds(pl.multiple_of(at, 128), size)


def lane_pick(table, index):
    return jnp.take_along_axis(table, index, axis=1)


LEFT_STEPS, RIGHT_STEPS = 17, 9
PAD = 384


def upsample_matrix(up_ref):
    row = lax.broadcasted_iota(i32, (16, 128), 0)
    lane = lax.broadcasted_iota(i32, (16, 128), 1)
    for pattern in range(2):
        for offset in range(6):
            gap = (32 * pattern + 30 + offset + (lane >> 2) - row).astype(f32).astype(bf16)
            one, zero = jnp.ones((16, 128), bf16), jnp.zeros((16, 128), bf16)
            for m in range(8):
                part = jnp.where(gap == jnp.full((16, 128), 16 * m, bf16), one, zero)
                at = (pattern * 6 + offset) * 128
                up_ref[16 * m : 16 * m + 16, at : at + 128] = part
                up_ref[128 + 16 * m : 144 + 16 * m, at : at + 128] = part


def spread_weights(stencil_ref, weight_ref, by_offset_ref, origin, count):
    row = lax.broadcasted_iota(i32, (8, 128), 0)
    lane = lax.broadcasted_iota(i32, (8, 128), 1)

    def step(block, _):
        weight = jnp.concatenate(
            [weight_ref[:, lanes(block * 128)], jnp.zeros((4, 128), f32)], axis=0
        )
        stencil = jnp.broadcast_to(stencil_ref[:, lanes(block * 128)], (8, 128))
        base = stencil - (origin + block * 32) - (lane >> 2)
        by_offset_ref[:, lanes(block * 128 + PAD)] = jnp.take_along_axis(
            weight, (row - 1 - base) & 7, axis=0
        )
        return 0

    lax.fori_loop(0, count // 128, step, 0, unroll=4)


def two_terms(value):
    top = value.astype(bf16)
    return top, (value - top.astype(f32)).astype(bf16)


def coarse_windows(coarse, lhs_ref, base, steps):
    def step(b, _):
        here = coarse((b + steps) % (steps + 1))
        after = coarse(b)
        mid = jnp.concatenate([here[:, 64:], after[:, :64]], axis=1)
        for w, window in enumerate((here, mid)):
            top, rest = two_terms(window)
            rows = pl.ds(pl.multiple_of(base + b * 64 + w * 32, 32), 32)
            lhs_ref[rows, 0:128] = top
            lhs_ref[rows, 128:256] = rest
        return 0

    lax.fori_loop(0, steps, step, 0)


def interpolate(lhs_ref, up_ref, by_offset_ref, fine_ref, base, steps):
    for tile in range(6):
        pattern, first = tile // 3, tile % 3 * 2
        got = jnp.dot(
            lhs_ref[base : base + steps * 64, :],
            up_ref[:, tile * 256 : tile * 256 + 256],
            preferred_element_type=f32,
        )
        for b in range(steps):
            for w in range(2):
                at = slice(b * 512 + (2 * w + pattern) * 128, b * 512 + (2 * w + pattern) * 128 + 128)
                weight = [
                    jnp.broadcast_to(by_offset_ref[first + n : first + n + 1, at], (8, 128))
                    for n in range(2)
                ]
                for g in range(4):
                    row = b * 64 + w * 32 + g * 8
                    part = got[row : row + 8, 0:128] * weight[0] + got[row : row + 8, 128:256] * weight[1]
                    if first:
                        part = part + fine_ref[8 * g : 8 * g + 8, at]
                    fine_ref[8 * g : 8 * g + 8, at] = part


def pick_columns(fine_ref, start, position):
    j = jnp.broadcast_to(position >> 7, (8, 128))
    lo = jnp.broadcast_to(position & 127, (8, 128))
    bits = [(j & (1 << b)) != 0 for b in range(5)]

    def tree(g, prefix, bit):
        if bit < 0:
            return lane_pick(fine_ref[8 * g : 8 * g + 8, lanes(PAD + start + prefix * 128)], lo)
        off = tree(g, prefix, bit - 1)
        on = tree(g, prefix | 1 << bit, bit - 1)
        return jnp.where(bits[bit], on, off)

    return [tree(g, 0, 4) for g in range(4)]


def build_table(fine_ref, table_ref):
    def step(hi, _):
        for h in range(2):
            j = (hi >> 1) * 4 + h * 2 + (hi & 1)
            for half in range(2):
                v = fine_ref[16 * half : 16 * half + 16, lanes(PAD + j * 128)]
                top, rest = two_terms(v)
                rows = pl.ds(pl.multiple_of(hi * 32 + 16 * half, 16), 16)
                rest_rows = pl.ds(pl.multiple_of(512 + hi * 32 + 16 * half, 16), 16)
                table_ref[rows, h * 128 : h * 128 + 128] = top
                table_ref[rest_rows, h * 128 : h * 128 + 128] = rest
        return 0

    lax.fori_loop(0, 16, step, 0, unroll=4)


def one_hot(lo):
    lo16 = jnp.broadcast_to(lo, (16, 128)) - lax.broadcasted_iota(i32, (16, 128), 0)
    lo16 = lo16.astype(f32).astype(bf16)
    one, zero = jnp.ones((16, 128), bf16), jnp.zeros((16, 128), bf16)
    return jnp.concatenate(
        [jnp.where(lo16 == jnp.full((16, 128), 16 * m, bf16), one, zero) for m in range(16)], axis=0
    )


def table_columns(table_ref, positions):
    split = [split_position(p, 4) for p in positions]
    hot = jnp.concatenate([one_hot(lo) for _, lo in split], axis=1)
    got = jnp.dot(table_ref[...], hot, preferred_element_type=f32)
    out = []
    for sub, (hi, _) in enumerate(split):
        hi8 = jnp.broadcast_to(hi, (8, 128))
        bits = [(hi8 & (1 << b)) != 0 for b in range(4)]

        def tree(g, prefix, bit):
            if bit < 0:
                row = prefix * 32 + 8 * g
                cut = slice(sub * 128, sub * 128 + 128)
                return got[row : row + 8, cut] + got[512 + row : 520 + row, cut]
            return jnp.where(bits[bit], tree(g, prefix | 1 << bit, bit - 1), tree(g, prefix, bit - 1))

        out.append([tree(g, 0, 3) for g in range(4)])
    return out


def sample_block(blk, fl_ref, table_ref, vl_ref, vr_ref, rows_ref, cols_ref, vals_ref, mask_ref):
    tile = blk // PER_TILE
    subs = [(blk % PER_TILE) * BLOCK + sub * 128 for sub in range(BLOCK // 128)]
    rights = table_columns(table_ref, [cols_ref[tile, :, lanes(at)] for at in subs])
    keep = mask_ref[0, tile].astype(f32) * -ETA
    for sub, at in enumerate(subs):
        left = pick_columns(fl_ref, tile * TILE, rows_ref[tile, :, lanes(at)])
        right = rights[sub]
        dots = (left[0] * right[0] + left[1] * right[1]) + (left[2] * right[2] + left[3] * right[3])
        error = jnp.sum(dots, axis=0, keepdims=True) - vals_ref[tile, :, lanes(at)]
        scaled = jnp.broadcast_to(error * keep, (8, 128))
        out = lanes(blk * BLOCK + sub * 128)
        for g in range(4):
            vl_ref[8 * g : 8 * g + 8, out] = scaled * right[g]
            vr_ref[8 * g : 8 * g + 8, out] = scaled * left[g]


def split_position(position, period):
    half = 8 // period
    j = position >> 7
    hi = (j // (2 * half)) * half + (j & (half - 1))
    lo = ((j // half) & 1) * 128 + (position & 127)
    return hi, lo


def scatter_block(blk, value_ref, position_ref, out_ref, period, place, at, part, parts):
    tile = blk // PER_TILE
    per_tile = 16 // period
    count = 16 // per_tile
    row16 = lax.broadcasted_iota(i32, (16, 128), 0)
    groups = range(4 * part // parts, 4 * (part + 1) // parts)
    hots, columns = [], []
    for sub in range(BLOCK // 128):
        position = position_ref[tile, :, lanes((blk % PER_TILE) * BLOCK + sub * 128)]
        hi, lo = split_position(position, period)
        hi16 = jnp.broadcast_to(hi, (16, 128)) - row16 // period
        masks = [jnp.where(hi16 == m * per_tile, 1.0, 0.0).astype(bf16) for m in range(count)]
        hots.append(one_hot(lo))
        top_rows, rest_rows = [], []
        for g in groups:
            v = value_ref[8 * g : 8 * g + 8, lanes(blk * BLOCK + sub * 128)]
            for first in range(0, 8, period):
                index = first + lax.broadcasted_iota(i32, (8, 128), 0) % period
                dup = jnp.take_along_axis(v, index, axis=0)
                top, rest = two_terms(jnp.concatenate([dup, dup], axis=0))
                top_rows += [top * mask for mask in masks]
                rest_rows += [rest * mask for mask in masks]
        columns.append(jnp.concatenate(top_rows + rest_rows, axis=0))
    lhs = jnp.concatenate(columns, axis=1)
    rhs = jnp.concatenate(hots, axis=1)
    got = lax.dot_general(lhs, rhs, (((1,), (1,)), ((), ())), preferred_element_type=f32)
    slots = 32 // period // parts
    each = 64 * period // 32
    for slot in range(slots):
        for g in range(each):
            for h in range(2):
                row = (slot * each + g) * 8
                cut = slice(h * 128, h * 128 + 128)
                rows = pl.ds(pl.multiple_of(at + g * 16 + h * 8, 8), 8)
                both = got[row : row + 8, cut] + got[512 // parts + row : 512 // parts + row + 8, cut]
                out_ref[place(part * slots + slot), rows, :] += both


def left_place(slot):
    return slot % 2 * 8 + slot // 2 % 4 * 2 + slot // 8


def right_place(slot):
    return slot


def add_own(fine_ref, out_ref, slot, period, place):
    group = pl.multiple_of((slot * period) // 8 * 8, 8)
    row = lax.broadcasted_iota(i32, (8, 128), 0)
    index = (slot * period) % 8 + row % period
    spread = 8 // period

    def step(block, _):
        got = None
        for q in range(spread):
            tall = fine_ref[pl.ds(group, 8), lanes(PAD + (block * spread + q) * 128)]
            picked = jnp.take_along_axis(tall, index, axis=0)
            got = picked if got is None else jnp.where(row // period == q, picked, got)
        out_ref[place(slot), pl.ds(pl.multiple_of(block * 8, 8), 8), :] = got
        return 0

    lax.fori_loop(0, 16, step, 0, unroll=4)


MESH_ID = pl.DeviceIdType.MESH


def gather_coarse(r, c, cl_ref, cr_ref, gl_ref, gr_ref, edges, mains, halos):
    def send(src, dst, sems, at, to):
        return pltpu.make_async_remote_copy(
            src_ref=src, dst_ref=dst, send_sem=sems[0].at[at], recv_sem=sems[1].at[at],
            device_id=to, device_id_type=MESH_ID,
        )

    col_peers = [(d, (r, (c + d) % 16)) for d in range(1, 16)]
    row_peers = [(15 + d, ((r + d) % 8, c)) for d in range(1, 8)]
    left_edges = [
        send(cl_ref.at[:, 0:128], gl_ref.at[c, :, 2048:2176], edges, 0, ((r + 7) % 8, c)),
        send(cl_ref.at[:, 1920:2048], gl_ref.at[c, :, 2176:2304], edges, 1, ((r + 1) % 8, c)),
    ]
    right_edges = [
        send(cr_ref.at[:, 0:128], gr_ref.at[r, :, 1024:1152], edges, 2, (r, (c + 15) % 16)),
        send(cr_ref.at[:, 896:1024], gr_ref.at[r, :, 1152:1280], edges, 3, (r, (c + 1) % 16)),
    ]
    left_mains = [send(cl_ref, gl_ref.at[c, :, 0:2048], mains, at, to) for at, to in col_peers]
    right_mains = [send(cr_ref, gr_ref.at[r, :, 0:1024], mains, at, to) for at, to in row_peers]
    own_left, own_right = gl_ref.at[c, :, 2048:2304], gr_ref.at[r, :, 1024:1280]
    left_halos = [send(own_left, own_left, halos, at, to) for at, to in col_peers]
    right_halos = [send(own_right, own_right, halos, at, to) for at, to in row_peers]

    def begin():
        for copy in left_edges + right_edges + right_mains + left_mains:
            copy.start()
        gl_ref[c, :, 0:2048] = cl_ref[...]
        gr_ref[r, :, 0:1024] = cr_ref[...]

    def forward():
        for copy in right_edges:
            copy.wait()
        for copy in right_halos:
            copy.start()
        for copy in left_edges:
            copy.wait()
        for copy in left_halos:
            copy.start()

    def end_right():
        for copy in right_mains + right_halos:
            copy.wait()

        @pl.when(c == 0)
        def _():
            gr_ref[:, :, 1152:1280] = jnp.zeros((8, 4, 128), f32)

        @pl.when(c == 15)
        def _():
            gr_ref[:, :, 1024:1152] = jnp.zeros((8, 4, 128), f32)

    def end_left():
        for copy in left_mains + left_halos:
            copy.wait()

        @pl.when(r == 0)
        def _():
            gl_ref[:, :, 2176:2304] = jnp.zeros((16, 2, 128), f32)

        @pl.when(r == 7)
        def _():
            gl_ref[:, :, 2048:2176] = jnp.zeros((16, 2, 128), f32)

    return begin, forward, end_right, end_left


class Exchange:
    def __init__(self, r, c, pl_ref, pr_ref, la_ref, lb_ref, ra_ref, rb_ref, work, sends, recvs):
        self.pair_ref, self.sum_ref, self.ly_ref, self.lsum_ref, self.rx_ref, self.rsum_ref = work
        self.pl_ref, self.pr_ref = pl_ref, pr_ref
        self.la_ref, self.lb_ref, self.ra_ref, self.rb_ref = la_ref, lb_ref, ra_ref, rb_ref
        self.sends, self.recvs = sends, recvs
        self.zlo, self.x = r // 4, r % 4
        self.zhi, self.y, self.core = c // 8, (c // 2) % 4, c % 2
        self.r, self.c = r, c

    def send(self, src, dst, at, to):
        return pltpu.make_async_remote_copy(
            src_ref=src, dst_ref=dst, send_sem=self.sends.at[at], recv_sem=self.recvs.at[at],
            device_id=to, device_id_type=MESH_ID,
        )

    def pair(self, p):
        cut = pl.ds(p * 64, 64)
        return self.send(
            self.pl_ref.at[pl.ds((1 - self.core) * 8, 8), cut], self.pair_ref.at[:, cut], p,
            (self.r, self.c + 1 - 2 * self.core),
        )

    def along_y(self, p):
        cut = pl.ds(p * 64, 64)
        out = []
        for d in range(1, 4):
            there = (self.y + d) % 4
            out.append(self.send(
                self.sum_ref.at[pl.ds(there * 2, 2), cut], self.ly_ref.at[d - 1, :, cut],
                2 + p * 3 + d - 1, (self.r, self.zhi * 8 + there * 2 + self.core),
            ))
        return out

    def left_z(self, p):
        cut = pl.ds(p * 64, 64)
        return self.send(
            self.lsum_ref.at[1 - self.zhi, cut], self.lb_ref.at[cut], 8 + p, (self.r, (self.c + 8) % 16)
        )

    def along_x(self, half):
        out = []
        for d in range(1, 4):
            there = (self.x + d) % 4
            out.append(self.send(
                self.pr_ref.at[half * 4 + there], self.rx_ref.at[half, d - 1],
                10 + half * 3 + d - 1, (self.zlo * 4 + there, self.c),
            ))
        return out

    def right_z(self):
        return self.send(
            self.rsum_ref.at[1 - self.zlo], self.rb_ref, 16, ((self.r + 4) % 8, self.c)
        )

    def after_pair(self, p):
        cut = pl.ds(p * 64, 64)
        self.pair(p).wait()
        for s in range(8):
            self.sum_ref[s, cut] = self.pl_ref[self.core * 8 + s, cut] + self.pair_ref[s, cut]
        for copy in self.along_y(p):
            copy.start()

    def after_y(self, p):
        cut = pl.ds(p * 64, 64)
        for copy in self.along_y(p):
            copy.wait()
        for s in range(2):
            self.lsum_ref[s, cut] = self.sum_ref[self.y * 2 + s, cut] + (
                self.ly_ref[0, s, cut] + self.ly_ref[1, s, cut] + self.ly_ref[2, s, cut]
            )
        self.left_z(p).start()

    def after_x(self, half):
        for copy in self.along_x(half):
            copy.wait()
        self.rsum_ref[half] = self.pr_ref[half * 4 + self.x] + (
            self.rx_ref[half, 0] + self.rx_ref[half, 1] + self.rx_ref[half, 2]
        )

        @pl.when(self.zlo == 1 - half)
        def _():
            self.right_z().start()

    def end(self):
        self.la_ref[...] = self.lsum_ref[self.zhi]
        self.ra_ref[...] = self.rsum_ref[self.zlo]
        self.right_z().wait()
        for p in range(2):
            self.left_z(p).wait()


def step_kernel(
    mask_ref, cl_ref, cr_ref, sl_ref, wl_ref, sr_ref, wr_ref, rows_ref, cols_ref, vals_ref,
    la_ref, lb_ref, ra_ref, rb_ref,
    gl_ref, gr_ref, fl_ref, fr_ref, wl6_ref, wr6_ref, vl_ref, vr_ref, pl_ref, pr_ref,
    pair_ref, sum_ref, ly_ref, lsum_ref, rx_ref, rsum_ref,
    edge_send, edge_recv, main_send, main_recv, halo_send, halo_recv, sends, recvs,
):
    r = lax.axis_index("row")
    c = lax.axis_index("col")
    peers = [(r, (c + d) % 16) for d in range(1, 16)] + [((r + d) % 8, c) for d in range(1, 8)]
    barrier = pltpu.get_barrier_semaphore()
    for peer in peers:
        pl.semaphore_signal(barrier, inc=1, device_id=peer, device_id_type=MESH_ID)
    begin, forward, end_right, end_left = gather_coarse(
        r, c, cl_ref, cr_ref, gl_ref, gr_ref,
        (edge_send, edge_recv), (main_send, main_recv), (halo_send, halo_recv),
    )
    exchange = Exchange(
        r, c, pl_ref, pr_ref, la_ref, lb_ref, ra_ref, rb_ref,
        (pair_ref, sum_ref, ly_ref, lsum_ref, rx_ref, rsum_ref), sends, recvs,
    )

    def local(up_ref, lhs_ref, table_ref):
        spread_weights(sr_ref, wr_ref, wr6_ref, c * 1024, 4096)
        upsample_matrix(up_ref)
        pl.semaphore_wait(barrier, len(peers))
        begin()
        spread_weights(sl_ref, wl_ref, wl6_ref, r * 2048, 8192)
        forward()
        pl_ref[...] = jnp.zeros(pl_ref.shape, f32)
        pr_ref[...] = jnp.zeros(pr_ref.shape, f32)
        end_right()
        right_base = LEFT_STEPS * 64
        coarse_windows(
            lambda b: gr_ref[:, :, lanes(b * 128)].reshape(32, 128), lhs_ref, right_base, RIGHT_STEPS
        )
        interpolate(lhs_ref, up_ref, wr6_ref, fr_ref, right_base, RIGHT_STEPS)
        build_table(fr_ref, table_ref)
        add_own(fr_ref, pr_ref, r, 4, right_place)
        end_left()
        coarse_windows(lambda b: gl_ref[:, :, lanes(b * 128)].reshape(32, 128), lhs_ref, 0, LEFT_STEPS)
        interpolate(lhs_ref, up_ref, wl6_ref, fl_ref, 0, LEFT_STEPS)
        add_own(fl_ref, pl_ref, c, 2, left_place)

        def sample(blk):
            sample_block(blk, fl_ref, table_ref, vl_ref, vr_ref, rows_ref, cols_ref, vals_ref, mask_ref)

        def scatter_left(blk):
            scatter_block(blk, vl_ref, rows_ref, pl_ref, 2, left_place, blk // PER_TILE * 64, 0, 1)

        sample(0)

        @pl.loop(1, BLOCKS)
        def _(blk):
            scatter_left(blk - 1)
            sample(blk)

            @pl.when(blk == PER_TILE)
            def _():
                exchange.pair(0).start()

            @pl.when(blk == PER_TILE + 2)
            def _():
                exchange.after_pair(0)

        scatter_left(BLOCKS - 1)
        exchange.pair(1).start()

        @pl.loop(0, BLOCKS)
        def _(blk):
            scatter_block(blk, vr_ref, cols_ref, pr_ref, 4, right_place, 0, 0, 2)

            @pl.when(blk == BLOCKS - 1)
            def _():
                exchange.after_pair(1)

        for copy in exchange.along_x(0):
            copy.start()

        @pl.loop(0, BLOCKS)
        def _(blk):
            scatter_block(blk, vr_ref, cols_ref, pr_ref, 4, right_place, 0, 1, 2)

            @pl.when(blk == BLOCKS // 2)
            def _():
                exchange.after_y(0)

        for copy in exchange.along_x(1):
            copy.start()
        exchange.after_x(0)
        exchange.after_y(1)
        exchange.after_x(1)
        exchange.end()

    pl.run_scoped(
        local,
        pltpu.VMEM((256, 1536), bf16),
        pltpu.VMEM(((LEFT_STEPS + RIGHT_STEPS) * 64, 256), bf16),
        pltpu.VMEM((1024, 256), bf16),
    )


def on_device(coarse_left, coarse_right, sl, wl, sr, wr, mask, rows, cols, vals):
    vmem = pl.BlockSpec(memory_space=pltpu.VMEM)
    smem = pl.BlockSpec(memory_space=pltpu.SMEM)
    dma = pltpu.SemaphoreType.DMA
    block = (128, 128)
    la, lb, ra, rb = pl.pallas_call(
        step_kernel,
        out_shape=(jax.ShapeDtypeStruct(block, f32),) * 4,
        in_specs=[smem] + [vmem] * 9,
        out_specs=(vmem,) * 4,
        scratch_shapes=[
            pltpu.VMEM((16, 2, 2304), f32),
            pltpu.VMEM((8, 4, 1280), f32),
            pltpu.VMEM((32, 512 * LEFT_STEPS), f32),
            pltpu.VMEM((32, 512 * RIGHT_STEPS), f32),
            pltpu.VMEM((8, 512 * LEFT_STEPS), f32),
            pltpu.VMEM((8, 512 * RIGHT_STEPS), f32),
            pltpu.VMEM((32, 2 * SPT), f32),
            pltpu.VMEM((32, 2 * SPT), f32),
            pltpu.VMEM((16, *block), f32),
            pltpu.VMEM((8, *block), f32),
            pltpu.VMEM((8, *block), f32),
            pltpu.VMEM((8, *block), f32),
            pltpu.VMEM((3, 2, *block), f32),
            pltpu.VMEM((2, *block), f32),
            pltpu.VMEM((2, 3, *block), f32),
            pltpu.VMEM((2, *block), f32),
            dma((4,)), dma((4,)), dma((23,)), dma((23,)), dma((23,)), dma((23,)),
            dma((17,)), dma((17,)),
        ],
        compiler_params=pltpu.CompilerParams(collective_id=0, has_side_effects=True),
        name="fused_step",
    )(
        mask.reshape(1, 2), coarse_left, coarse_right, sl.reshape(1, -1), wl, sr.reshape(1, -1), wr,
        rows, cols, vals,
    )
    left_new = (la + lb).reshape(64, 2, 128).transpose(1, 0, 2).reshape(2, 8192)
    right_new = (ra + rb).reshape(32, 4, 128).transpose(1, 0, 2).reshape(4, 4096)
    return left_new, right_new


def solution(mesh):
    in_specs = (
        P("col", "row"),
        P("row", "col"),
        P("row"),
        P(None, "row"),
        P("col"),
        P(None, "col"),
        P("row", "col"),
        P("row", "col", None),
        P("row", "col", None),
        P("row", "col", None),
    )
    out_specs = (P("col", "row"), P("row", "col"))
    return jax.shard_map(
        on_device, mesh=mesh, in_specs=in_specs, out_specs=out_specs, check_vma=False
    )
```

time: 50.2 us -> 45.8 us (0.912)
  Pallas kernels: 47.3 us -> 42.5 us
  other arithmetic: 0 us -> 2.18 us
  local copies, waits for them, and re-layouts: 2.14 us -> 0.01 us
    pallas_call x1, Pallas kernels: 47.3 us -> 42.5 us  [on_device(): pl.pallas_call(step_kernel, out_shape=(jax.ShapeDtypeStruct(block, f32),)...]
    add x0 -> x2, other arithmetic: none -> 2.18 us  [the longest x1 1.54 us: on_device(): left_new = (la + lb).reshape(64, 2, 128).transpose(1, 0, 2).reshape(2, 8192)]
    unnamed x4, local copies, waits for them, and re-layouts: 2.14 us -> 0.01 us
where the time goes in v4:
time: 45.8 us; the launch traced here: 45.3 us
  Pallas kernels  42.5 us (93%)
  other arithmetic  2.18 us (5%)
  between operations  0.66 us (1%)
    pallas_call x1, Pallas kernels, on_device(): pl.pallas_call(step_kernel, out_shape=(jax.ShapeDtypeStruct(block, f32),)...  42.5 us
    add x1, other arithmetic, on_device(): left_new = (la + lb).reshape(64, 2, 128).transpose(1, 0, 2).reshape(2, 8192)  1.54 us

profile of v4, /device:TPU:0, one launch (start us, length us, event | category | flops | bytes accessed | tf_op | source)
XLA Modules:
  0.0 45.3 jit_solution(333814950961810944)
XLA Ops:
  0.6 42.5 %fused_step.1 = (f32[128,128]{1,0:T(8,128)}, f32[128,128]{1,0:T(8,128)}, f32[128,128]{1,0:T(8,128)}, f32[128,128]{1,0:T(8,128)}) custom-call(s32[1,2]{1,0:T(1,128)} %bitcast.17, f32[2,2048]{1,0:T(2,128)} %cl_ref.1, f32[4,1024]{1,0:T(4,128)} %cr_ref.1, s32[1,8192]{1,0:T(1,128)} %bitcast.15, f32[4,8192]{1,0:T(4,128)} %wl_ref.1, s32[1,4096]{1,0:T(1,128)} %bitcast.16, ...), custom_call_target="tpu_custom_call" | custom-call | tf_op jit(solution)/shard_map/fused_step/pallas_call | solution.py:521
  43.1 0.0 copy-start
  43.1 0.0 copy-start.1
  43.2 1.5 %add.6 = f32[128,128]{1,0:T(8,128)} add(f32[128,128]{1,0:T(8,128)} %get-tuple-element.6, f32[128,128]{1,0:T(8,128)} %get-tuple-element.7) | non-fusion elementwise | flops 16384 | bytes 196608 | tf_op jit(solution)/shard_map/add | solution.py:552
  44.7 0.0 copy-done
  44.7 0.0 copy-done.1
  44.7 0.6 %add.7 = f32[128,128]{1,0:T(8,128)} add(f32[128,128]{1,0:T(8,128)S(1)} %copy-done, f32[128,128]{1,0:T(8,128)S(1)} %copy-done.1) | non-fusion elementwise | flops 16384 | bytes 196608 | tf_op jit(solution)/shard_map/add | solution.py:553
Async XLA Ops:
  43.1 1.6 %copy-start = (f32[128,128]{1,0:T(8,128)S(1)}, f32[128,128]{1,0:T(8,128)}, u32[]{:S(2)}) copy-start(f32[128,128]{1,0:T(8,128)} %get-tuple-element.8) | copy-start | bytes 196612
  43.1 1.6 %copy-start.1 = (f32[128,128]{1,0:T(8,128)S(1)}, f32[128,128]{1,0:T(8,128)}, u32[]{:S(2)}) copy-start(f32[128,128]{1,0:T(8,128)} %get-tuple-element.9) | copy-start | bytes 196612

commit v5 on v4

--- a/solution.py
+++ b/solution.py
@@ -64,18 +64,16 @@
 
 
 def coarse_windows(coarse, lhs_ref, base, steps):
-    def step(b, _):
-        here = coarse((b + steps) % (steps + 1))
+    here = coarse(steps)
+    for b in range(steps):
         after = coarse(b)
         mid = jnp.concatenate([here[:, 64:], after[:, :64]], axis=1)
         for w, window in enumerate((here, mid)):
             top, rest = two_terms(window)
-            rows = pl.ds(pl.multiple_of(base + b * 64 + w * 32, 32), 32)
+            rows = slice(base + b * 64 + w * 32, base + b * 64 + w * 32 + 32)
             lhs_ref[rows, 0:128] = top
             lhs_ref[rows, 128:256] = rest
-        return 0
-
-    lax.fori_loop(0, steps, step, 0)
+        here = after
 
 
 def interpolate(lhs_ref, up_ref, by_offset_ref, fine_ref, base, steps):
@@ -141,12 +139,30 @@
     )
 
 
-def table_columns(table_ref, positions):
-    split = [split_position(p, 4) for p in positions]
-    hot = jnp.concatenate([one_hot(lo) for _, lo in split], axis=1)
+def index_tables(position_ref, hot_ref, hi_ref, period):
+    per_tile = 16 // period
+    row16 = lax.broadcasted_iota(i32, (16, 128), 0)
+
+    for tile in range(2):
+        def step(n, _):
+            hi, lo = split_position(position_ref[tile, :, lanes(n * 128)], period)
+            at = lanes(tile * SPT + n * 128)
+            hot_ref[:, at] = one_hot(lo)
+            hi16 = (jnp.broadcast_to(hi, (16, 128)) - row16 // period).astype(f32).astype(bf16)
+            one, zero = jnp.ones((16, 128), bf16), jnp.zeros((16, 128), bf16)
+            for m in range(period):
+                same = hi16 == jnp.full((16, 128), m * per_tile, bf16)
+                hi_ref[16 * m : 16 * m + 16, at] = jnp.where(same, one, zero)
+            return 0
+
+        lax.fori_loop(0, SPT // 128, step, 0, unroll=2)
+
+
+def table_columns(table_ref, hot, positions):
     got = jnp.dot(table_ref[...], hot, preferred_element_type=f32)
     out = []
-    for sub, (hi, _) in enumerate(split):
+    for sub, position in enumerate(positions):
+        hi, _ = split_position(position, 4)
         hi8 = jnp.broadcast_to(hi, (8, 128))
         bits = [(hi8 & (1 << b)) != 0 for b in range(4)]
 
@@ -161,10 +177,11 @@
     return out
 
 
-def sample_block(blk, fl_ref, table_ref, vl_ref, vr_ref, rows_ref, cols_ref, vals_ref, mask_ref):
+def sample_block(blk, fl_ref, table_ref, hot_ref, vl_ref, vr_ref, rows_ref, cols_ref, vals_ref, mask_ref):
     tile = blk // PER_TILE
     subs = [(blk % PER_TILE) * BLOCK + sub * 128 for sub in range(BLOCK // 128)]
-    rights = table_columns(table_ref, [cols_ref[tile, :, lanes(at)] for at in subs])
+    hot = hot_ref[:, lanes(blk * BLOCK, BLOCK)]
+    rights = table_columns(table_ref, hot, [cols_ref[tile, :, lanes(at)] for at in subs])
     keep = mask_ref[0, tile].astype(f32) * -ETA
     for sub, at in enumerate(subs):
         left = pick_columns(fl_ref, tile * TILE, rows_ref[tile, :, lanes(at)])
@@ -186,22 +203,15 @@
     return hi, lo
 
 
-def scatter_block(blk, value_ref, position_ref, out_ref, period, place, at, part, parts):
-    tile = blk // PER_TILE
-    per_tile = 16 // period
-    count = 16 // per_tile
-    row16 = lax.broadcasted_iota(i32, (16, 128), 0)
+def scatter_block(first_sample, samples, value_ref, hot_ref, hi_ref, out_ref, period, place, at, part, parts):
     groups = range(4 * part // parts, 4 * (part + 1) // parts)
-    hots, columns = [], []
-    for sub in range(BLOCK // 128):
-        position = position_ref[tile, :, lanes((blk % PER_TILE) * BLOCK + sub * 128)]
-        hi, lo = split_position(position, period)
-        hi16 = jnp.broadcast_to(hi, (16, 128)) - row16 // period
-        masks = [jnp.where(hi16 == m * per_tile, 1.0, 0.0).astype(bf16) for m in range(count)]
-        hots.append(one_hot(lo))
+    columns = []
+    for sub in range(samples // 128):
+        here = lanes(first_sample + sub * 128)
+        masks = [hi_ref[16 * m : 16 * m + 16, here] for m in range(period)]
         top_rows, rest_rows = [], []
         for g in groups:
-            v = value_ref[8 * g : 8 * g + 8, lanes(blk * BLOCK + sub * 128)]
+            v = value_ref[8 * g : 8 * g + 8, here]
             for first in range(0, 8, period):
                 index = first + lax.broadcasted_iota(i32, (8, 128), 0) % period
                 dup = jnp.take_along_axis(v, index, axis=0)
@@ -210,7 +220,7 @@
                 rest_rows += [rest * mask for mask in masks]
         columns.append(jnp.concatenate(top_rows + rest_rows, axis=0))
     lhs = jnp.concatenate(columns, axis=1)
-    rhs = jnp.concatenate(hots, axis=1)
+    rhs = hot_ref[:, lanes(first_sample, samples)]
     got = lax.dot_general(lhs, rhs, (((1,), (1,)), ((), ())), preferred_element_type=f32)
     slots = 32 // period // parts
     each = 64 * period // 32
@@ -433,13 +443,15 @@
         (pair_ref, sum_ref, ly_ref, lsum_ref, rx_ref, rsum_ref), sends, recvs,
     )
 
-    def local(up_ref, lhs_ref, table_ref):
+    def local(up_ref, lhs_ref, table_ref, hotr_ref, hotc_ref, hir_ref, hic_ref):
         spread_weights(sr_ref, wr_ref, wr6_ref, c * 1024, 4096)
         upsample_matrix(up_ref)
+        spread_weights(sl_ref, wl_ref, wl6_ref, r * 2048, 8192)
         pl.semaphore_wait(barrier, len(peers))
         begin()
-        spread_weights(sl_ref, wl_ref, wl6_ref, r * 2048, 8192)
+        index_tables(cols_ref, hotc_ref, hic_ref, 4)
         forward()
+        index_tables(rows_ref, hotr_ref, hir_ref, 2)
         pl_ref[...] = jnp.zeros(pl_ref.shape, f32)
         pr_ref[...] = jnp.zeros(pr_ref.shape, f32)
         end_right()
@@ -456,16 +468,24 @@
         add_own(fl_ref, pl_ref, c, 2, left_place)
 
         def sample(blk):
-            sample_block(blk, fl_ref, table_ref, vl_ref, vr_ref, rows_ref, cols_ref, vals_ref, mask_ref)
-
-        def scatter_left(blk):
-            scatter_block(blk, vl_ref, rows_ref, pl_ref, 2, left_place, blk // PER_TILE * 64, 0, 1)
+            sample_block(
+                blk, fl_ref, table_ref, hotc_ref, vl_ref, vr_ref, rows_ref, cols_ref, vals_ref, mask_ref
+            )
+
+        def scatter(blk):
+            at = blk // PER_TILE * 64
+            scatter_block(
+                blk * BLOCK, BLOCK, vl_ref, hotr_ref, hir_ref, pl_ref, 2, left_place, at, 0, 1
+            )
+            scatter_block(
+                blk * BLOCK, BLOCK, vr_ref, hotc_ref, hic_ref, pr_ref, 4, right_place, 0, 0, 2
+            )
 
         sample(0)
 
         @pl.loop(1, BLOCKS)
         def _(blk):
-            scatter_left(blk - 1)
+            scatter(blk - 1)
             sample(blk)
 
             @pl.when(blk == PER_TILE)
@@ -476,30 +496,24 @@
             def _():
                 exchange.after_pair(0)
 
-        scatter_left(BLOCKS - 1)
+        scatter(BLOCKS - 1)
         exchange.pair(1).start()
-
-        @pl.loop(0, BLOCKS)
-        def _(blk):
-            scatter_block(blk, vr_ref, cols_ref, pr_ref, 4, right_place, 0, 0, 2)
-
-            @pl.when(blk == BLOCKS - 1)
+        for copy in exchange.along_x(0):
+            copy.start()
+
+        @pl.loop(0, BLOCKS // 2)
+        def _(step):
+            scatter_block(
+                step * 2 * BLOCK, 2 * BLOCK, vr_ref, hotc_ref, hic_ref, pr_ref, 4, right_place, 0, 1, 2
+            )
+
+            @pl.when(step == BLOCKS // 2 - 1)
             def _():
                 exchange.after_pair(1)
 
-        for copy in exchange.along_x(0):
-            copy.start()
-
-        @pl.loop(0, BLOCKS)
-        def _(blk):
-            scatter_block(blk, vr_ref, cols_ref, pr_ref, 4, right_place, 0, 1, 2)
-
-            @pl.when(blk == BLOCKS // 2)
-            def _():
-                exchange.after_y(0)
-
         for copy in exchange.along_x(1):
             copy.start()
+        exchange.after_y(0)
         exchange.after_x(0)
         exchange.after_y(1)
         exchange.after_x(1)
@@ -510,7 +524,16 @@
         pltpu.VMEM((256, 1536), bf16),
         pltpu.VMEM(((LEFT_STEPS + RIGHT_STEPS) * 64, 256), bf16),
         pltpu.VMEM((1024, 256), bf16),
+        pltpu.VMEM((256, 2 * SPT), bf16),
+        pltpu.VMEM((256, 2 * SPT), bf16),
+        pltpu.VMEM((32, 2 * SPT), bf16),
+        pltpu.VMEM((64, 2 * SPT), bf16),
     )
+
+
+def finish_kernel(la_ref, lb_ref, ra_ref, rb_ref, left_ref, right_ref):
+    left_ref[...] = la_ref[...] + lb_ref[...]
+    right_ref[...] = ra_ref[...] + rb_ref[...]
 
 
 def on_device(coarse_left, coarse_right, sl, wl, sr, wr, mask, rows, cols, vals):
@@ -549,8 +572,15 @@
         mask.reshape(1, 2), coarse_left, coarse_right, sl.reshape(1, -1), wl, sr.reshape(1, -1), wr,
         rows, cols, vals,
     )
-    left_new = (la + lb).reshape(64, 2, 128).transpose(1, 0, 2).reshape(2, 8192)
-    right_new = (ra + rb).reshape(32, 4, 128).transpose(1, 0, 2).reshape(4, 4096)
+    left_sum, right_sum = pl.pallas_call(
+        finish_kernel,
+        out_shape=(jax.ShapeDtypeStruct(block, f32),) * 2,
+        in_specs=[vmem] * 4,
+        out_specs=(vmem,) * 2,
+        name="finish",
+    )(la, lb, ra, rb)
+    left_new = left_sum.reshape(64, 2, 128).transpose(1, 0, 2).reshape(2, 8192)
+    right_new = right_sum.reshape(32, 4, 128).transpose(1, 0, 2).reshape(4, 4096)
     return left_new, right_new
 
 

time: 45.8 us -> 42.6 us (0.930)
  other arithmetic: 2.18 us -> 0 us
  Pallas kernels: 42.5 us -> 41.8 us
    pallas_call x1, Pallas kernels: 42.5 us -> 40.2 us  [on_device(): pl.pallas_call(step_kernel, out_shape=(jax.ShapeDtypeStruct(block, f32),)...]
    add x2 -> x0, other arithmetic: 2.18 us -> none  [the longest x1 1.54 us: on_device(): left_new = (la + lb).reshape(64, 2, 128).transpose(1, 0, 2).reshape(2, 8192)]
    pallas_call x0 -> x1, Pallas kernels: none -> 1.6 us  [on_device(): pl.pallas_call(finish_kernel, out_shape=(jax.ShapeDtypeStruct(block, f32)...]
where the time goes in v5:
time: 42.6 us; the launch traced here: 42.4 us
  Pallas kernels  41.8 us (98%)
  between operations  0.64 us (2%)
    pallas_call x1, Pallas kernels, on_device(): pl.pallas_call(step_kernel, out_shape=(jax.ShapeDtypeStruct(block, f32),)...  40.2 us
    pallas_call x1, Pallas kernels, on_device(): pl.pallas_call(finish_kernel, out_shape=(jax.ShapeDtypeStruct(block, f32)...  1.6 us

profile of v5, /device:TPU:0, one launch (start us, length us, event | category | flops | bytes accessed | tf_op | source)
XLA Modules:
  0.0 42.4 jit_solution(15888798326200351258)
XLA Ops:
  0.6 40.2 %fused_step.1 = (f32[128,128]{1,0:T(8,128)}, f32[128,128]{1,0:T(8,128)}, f32[128,128]{1,0:T(8,128)}, f32[128,128]{1,0:T(8,128)}) custom-call(s32[1,2]{1,0:T(1,128)} %bitcast.15, f32[2,2048]{1,0:T(2,128)} %cl_ref.1, f32[4,1024]{1,0:T(4,128)} %cr_ref.1, s32[1,8192]{1,0:T(1,128)} %bitcast.13, f32[4,8192]{1,0:T(4,128)} %wl_ref.1, s32[1,4096]{1,0:T(1,128)} %bitcast.14, ...), custom_call_target="tpu_custom_call" | custom-call | tf_op jit(solution)/shard_map/fused_step/pallas_call | solution.py:544
  40.8 1.6 %finish.1 = (f32[128,128]{1,0:T(8,128)}, f32[128,128]{1,0:T(8,128)}) custom-call(f32[128,128]{1,0:T(8,128)} %get-tuple-element.8.la_ref, f32[128,128]{1,0:T(8,128)} %get-tuple-element.9.lb_ref, f32[128,128]{1,0:T(8,128)} %get-tuple-element.10.ra_ref, f32[128,128]{1,0:T(8,128)} %get-tuple-element.11.rb_ref), custom_call_target="tpu_custom_call" | custom-call | tf_op jit(solution)/shard_map/finish/pallas_call | solution.py:575

commit v6 on v5

--- a/solution.py
+++ b/solution.py
@@ -330,11 +330,11 @@
 
 
 class Exchange:
-    def __init__(self, r, c, pl_ref, pr_ref, la_ref, lb_ref, ra_ref, rb_ref, work, sends, recvs):
+    def __init__(self, r, c, pl_ref, pr_ref, la_ref, lb_ref, ra_ref, rb_ref, work, sends, recvs, out_sem):
         self.pair_ref, self.sum_ref, self.ly_ref, self.lsum_ref, self.rx_ref, self.rsum_ref = work
         self.pl_ref, self.pr_ref = pl_ref, pr_ref
         self.la_ref, self.lb_ref, self.ra_ref, self.rb_ref = la_ref, lb_ref, ra_ref, rb_ref
-        self.sends, self.recvs = sends, recvs
+        self.sends, self.recvs, self.out_sem = sends, recvs, out_sem
         self.zlo, self.x = r // 4, r % 4
         self.zhi, self.y, self.core = c // 8, (c // 2) % 4, c % 2
         self.r, self.c = r, c
@@ -413,17 +413,26 @@
         def _():
             self.right_z().start()
 
+    def own(self):
+        return (
+            pltpu.make_async_copy(self.lsum_ref.at[self.zhi], self.la_ref, self.out_sem.at[0]),
+            pltpu.make_async_copy(self.rsum_ref.at[self.zlo], self.ra_ref, self.out_sem.at[1]),
+        )
+
     def end(self):
-        self.la_ref[...] = self.lsum_ref[self.zhi]
-        self.ra_ref[...] = self.rsum_ref[self.zlo]
+        for copy in self.own():
+            copy.start()
+        self.left_z(0).wait()
+        self.left_z(1).wait()
         self.right_z().wait()
-        for p in range(2):
-            self.left_z(p).wait()
+        for copy in self.own():
+            copy.wait()
 
 
 def step_kernel(
-    mask_ref, cl_ref, cr_ref, sl_ref, wl_ref, sr_ref, wr_ref, rows_ref, cols_ref, vals_ref,
+    mask_in, cl_in, cr_in, sl_in, wl_in, sr_in, wr_in, rows_in, cols_in, vals_in,
     la_ref, lb_ref, ra_ref, rb_ref,
+    mask_ref, cl_ref, cr_ref, sl_ref, wl_ref, sr_ref, wr_ref, rows_ref, cols_ref, vals_ref, in_sem, out_sem,
     gl_ref, gr_ref, fl_ref, fr_ref, wl6_ref, wr6_ref, vl_ref, vr_ref, pl_ref, pr_ref,
     pair_ref, sum_ref, ly_ref, lsum_ref, rx_ref, rsum_ref,
     edge_send, edge_recv, main_send, main_recv, halo_send, halo_recv, sends, recvs,
@@ -434,18 +443,27 @@
     barrier = pltpu.get_barrier_semaphore()
     for peer in peers:
         pl.semaphore_signal(barrier, inc=1, device_id=peer, device_id_type=MESH_ID)
+    pairs = (
+        (sr_in, sr_ref), (wr_in, wr_ref), (sl_in, sl_ref), (wl_in, wl_ref), (cl_in, cl_ref), (cr_in, cr_ref),
+        (cols_in, cols_ref), (rows_in, rows_ref), (vals_in, vals_ref), (mask_in, mask_ref),
+    )
+    loads = [pltpu.make_async_copy(src, dst, in_sem.at[n]) for n, (src, dst) in enumerate(pairs)]
+    for load in loads:
+        load.start()
     begin, forward, end_right, end_left = gather_coarse(
         r, c, cl_ref, cr_ref, gl_ref, gr_ref,
         (edge_send, edge_recv), (main_send, main_recv), (halo_send, halo_recv),
     )
     exchange = Exchange(
         r, c, pl_ref, pr_ref, la_ref, lb_ref, ra_ref, rb_ref,
-        (pair_ref, sum_ref, ly_ref, lsum_ref, rx_ref, rsum_ref), sends, recvs,
+        (pair_ref, sum_ref, ly_ref, lsum_ref, rx_ref, rsum_ref), sends, recvs, out_sem,
     )
 
     def local(up_ref, lhs_ref, table_ref, hotr_ref, hotc_ref, hir_ref, hic_ref):
+        upsample_matrix(up_ref)
+        for load in loads:
+            load.wait()
         spread_weights(sr_ref, wr_ref, wr6_ref, c * 1024, 4096)
-        upsample_matrix(up_ref)
         spread_weights(sl_ref, wl_ref, wl6_ref, r * 2048, 8192)
         pl.semaphore_wait(barrier, len(peers))
         begin()
@@ -507,7 +525,7 @@
                 step * 2 * BLOCK, 2 * BLOCK, vr_ref, hotc_ref, hic_ref, pr_ref, 4, right_place, 0, 1, 2
             )
 
-            @pl.when(step == BLOCKS // 2 - 1)
+            @pl.when(step == BLOCKS // 2 - 2)
             def _():
                 exchange.after_pair(1)
 
@@ -538,15 +556,23 @@
 
 def on_device(coarse_left, coarse_right, sl, wl, sr, wr, mask, rows, cols, vals):
     vmem = pl.BlockSpec(memory_space=pltpu.VMEM)
-    smem = pl.BlockSpec(memory_space=pltpu.SMEM)
+    anywhere = pl.BlockSpec(memory_space=pl.ANY)
+    operands = (
+        mask.reshape(1, 2), coarse_left, coarse_right, sl.reshape(1, -1), wl, sr.reshape(1, -1), wr,
+        rows, cols, vals,
+    )
     dma = pltpu.SemaphoreType.DMA
     block = (128, 128)
     la, lb, ra, rb = pl.pallas_call(
         step_kernel,
         out_shape=(jax.ShapeDtypeStruct(block, f32),) * 4,
-        in_specs=[smem] + [vmem] * 9,
-        out_specs=(vmem,) * 4,
+        in_specs=[anywhere] * 10,
+        out_specs=(anywhere,) * 4,
         scratch_shapes=[
+            pltpu.SMEM((1, 2), i32),
+            *[pltpu.VMEM(a.shape, a.dtype) for a in operands[1:]],
+            dma((10,)),
+            dma((2,)),
             pltpu.VMEM((16, 2, 2304), f32),
             pltpu.VMEM((8, 4, 1280), f32),
             pltpu.VMEM((32, 512 * LEFT_STEPS), f32),
@@ -568,10 +594,7 @@
         ],
         compiler_params=pltpu.CompilerParams(collective_id=0, has_side_effects=True),
         name="fused_step",
-    )(
-        mask.reshape(1, 2), coarse_left, coarse_right, sl.reshape(1, -1), wl, sr.reshape(1, -1), wr,
-        rows, cols, vals,
-    )
+    )(*operands)
     left_sum, right_sum = pl.pallas_call(
         finish_kernel,
         out_shape=(jax.ShapeDtypeStruct(block, f32),) * 2,

time: 42.6 us -> 40.7 us (0.955)
  Pallas kernels: 41.8 us -> 39.9 us
    pallas_call x1, Pallas kernels: 40.2 us -> 38.3 us  [on_device(): pl.pallas_call(step_kernel, out_shape=(jax.ShapeDtypeStruct(block, f32),)...]
where the time goes in v6:
time: 40.7 us; the launch traced here: 40.6 us
  Pallas kernels  39.9 us (98%)
  between operations  0.64 us (2%)
    pallas_call x1, Pallas kernels, on_device(): pl.pallas_call(step_kernel, out_shape=(jax.ShapeDtypeStruct(block, f32),)...  38.3 us
    pallas_call x1, Pallas kernels, on_device(): pl.pallas_call(finish_kernel, out_shape=(jax.ShapeDtypeStruct(block, f32)...  1.6 us

profile of v6, /device:TPU:0, one launch (start us, length us, event | category | flops | bytes accessed | tf_op | source)
XLA Modules:
  0.0 40.6 jit_solution(11385371254153408970)
XLA Ops:
  0.6 38.3 %fused_step.1 = (f32[128,128]{1,0:T(8,128)}, f32[128,128]{1,0:T(8,128)}, f32[128,128]{1,0:T(8,128)}, f32[128,128]{1,0:T(8,128)}) custom-call(s32[1,2]{1,0:T(1,128)} %bitcast.15, f32[2,2048]{1,0:T(2,128)} %cl_in.1, f32[4,1024]{1,0:T(4,128)} %cr_in.1, s32[1,8192]{1,0:T(1,128)} %bitcast.13, f32[4,8192]{1,0:T(4,128)} %wl_in.1, s32[1,4096]{1,0:T(1,128)} %bitcast.14, ...), custom_call_target="tpu_custom_call" | custom-call | tf_op jit(solution)/shard_map/fused_step/pallas_call | solution.py:566
  39.0 1.6 %finish.1 = (f32[128,128]{1,0:T(8,128)}, f32[128,128]{1,0:T(8,128)}) custom-call(f32[128,128]{1,0:T(8,128)} %get-tuple-element.8.la_ref, f32[128,128]{1,0:T(8,128)} %get-tuple-element.9.lb_ref, f32[128,128]{1,0:T(8,128)} %get-tuple-element.10.ra_ref, f32[128,128]{1,0:T(8,128)} %get-tuple-element.11.rb_ref), custom_call_target="tpu_custom_call" | custom-call | tf_op jit(solution)/shard_map/finish/pallas_call | solution.py:598

commit v7 on v6

--- a/solution.py
+++ b/solution.py
@@ -510,7 +510,7 @@
             def _():
                 exchange.pair(0).start()
 
-            @pl.when(blk == PER_TILE + 2)
+            @pl.when(blk == PER_TILE + 1)
             def _():
                 exchange.after_pair(0)
 

time: 40.7 us -> 41.2 us (1.012)
  Pallas kernels: 39.9 us -> 40.4 us
    pallas_call x1, Pallas kernels: 38.3 us -> 38.8 us  [on_device(): pl.pallas_call(step_kernel, out_shape=(jax.ShapeDtypeStruct(block, f32),)...]
where the time goes in v7:
time: 41.2 us; the launch traced here: 41.1 us
  Pallas kernels  40.4 us (98%)
  between operations  0.64 us (2%)
    pallas_call x1, Pallas kernels, on_device(): pl.pallas_call(step_kernel, out_shape=(jax.ShapeDtypeStruct(block, f32),)...  38.8 us
    pallas_call x1, Pallas kernels, on_device(): pl.pallas_call(finish_kernel, out_shape=(jax.ShapeDtypeStruct(block, f32)...  1.6 us

profile of v7, /device:TPU:0, one launch (start us, length us, event | category | flops | bytes accessed | tf_op | source)
XLA Modules:
  0.0 41.1 jit_solution(8145757459169041050)
XLA Ops:
  0.6 38.8 %fused_step.1 = (f32[128,128]{1,0:T(8,128)}, f32[128,128]{1,0:T(8,128)}, f32[128,128]{1,0:T(8,128)}, f32[128,128]{1,0:T(8,128)}) custom-call(s32[1,2]{1,0:T(1,128)} %bitcast.15, f32[2,2048]{1,0:T(2,128)} %cl_in.1, f32[4,1024]{1,0:T(4,128)} %cr_in.1, s32[1,8192]{1,0:T(1,128)} %bitcast.13, f32[4,8192]{1,0:T(4,128)} %wl_in.1, s32[1,4096]{1,0:T(1,128)} %bitcast.14, ...), custom_call_target="tpu_custom_call" | custom-call | tf_op jit(solution)/shard_map/fused_step/pallas_call | solution.py:566
  39.5 1.6 %finish.1 = (f32[128,128]{1,0:T(8,128)}, f32[128,128]{1,0:T(8,128)}) custom-call(f32[128,128]{1,0:T(8,128)} %get-tuple-element.8.la_ref, f32[128,128]{1,0:T(8,128)} %get-tuple-element.9.lb_ref, f32[128,128]{1,0:T(8,128)} %get-tuple-element.10.ra_ref, f32[128,128]{1,0:T(8,128)} %get-tuple-element.11.rb_ref), custom_call_target="tpu_custom_call" | custom-call | tf_op jit(solution)/shard_map/finish/pallas_call | solution.py:598
